TPU v7x, 32 devices: a whole 2x2x4 slice. The times are simulated.
32 devices in a mesh: groups: 2 (over x), pen: 16 (over z, y, core).
Axes of the slice: x: 2, y: 2, z: 4, core: 2. Of those that a mesh axis runs over, the one named last changes fastest.
Arguments:
- point_feat: bfloat16 [64, 65536], P(None, ('groups', 'pen')), parts along dimension 1, may hold values from -6 to 6
- pair_kernel: bfloat16 [2048, 128, 128], P(('groups', 'pen')), parts along dimension 0, may hold values from -0.5 to 0.5
- pair_owner: int32 [2048, 1], P(('groups', 'pen')), parts along dimension 0, may hold values from 0 to 15; in each aligned block of 64 rows (0 to 63, 64 to 127, ...) at most 8 rows name the same one
- pair_block: int32 [2048], P(('groups', 'pen')), parts along dimension 0, may hold values from 0 to 255
- spec_weight: bfloat16 [2, 256, 16, 64, 128], P(None, 'pen'), may hold values from -3 to 3
- mlp_up: bfloat16 [2, 256, 64], replicated, may hold values from -0.75 to 0.75
- mlp_down: bfloat16 [2, 64, 256], replicated, may hold values from -0.375 to 0.375
Outputs:
- point_out: float32 [64, 65536], P(None, ('groups', 'pen')), parts along dimension 1
There are 2 independent parts, one for each index of `groups`. A program takes and returns all parts, laid end to end along the dimension named above; an argument that names none is the same for every part. Nothing has to cross between parts.
Inputs may be any that keep to these rules, and one draw needn't show every extreme that they name: `pair_owner`: among the pairs of one device, no device is named more than 8 times.
All inputs are finite; a program needn't handle non-finite values.
Results may differ from a plain program's by a relative error of at most 0.0055.
Values may be sent and summed in bfloat16 or wider, within the bound.
A program may use at most 128 MiB of HBM per device.

v0:
```python
import functools
import math

import jax
import jax.numpy as jnp
import numpy as np
from jax import lax
from jax.experimental import pallas as pl
from jax.experimental.pallas import tpu as pltpu
from jax.sharding import PartitionSpec as P

NX = 128
NY = 64
NZ = 64
MX = 16
MY = 16
MZ = 16
LAYERS = 2
NBR = 4
NOTE_ROWS = 16

F32 = jnp.float32
BF16 = jnp.bfloat16
VMEM = pl.BlockSpec(memory_space=pltpu.VMEM)
SMEM = pl.BlockSpec(memory_space=pltpu.SMEM)
NT = (((1,), (1,)), ((), ()))


def plane_table(devices, lanes):
    here = MY * MZ // devices
    row = np.arange(2 * MY * MZ)
    mode = row // (2 * here) * here + row % here
    imag = (row % (2 * here)) // here
    wave_y = mode // MZ - MY // 2
    wave_z = mode % MZ
    cell = np.arange(lanes)
    turns = np.mod(np.outer(wave_y, cell // NZ), NY) / NY + np.mod(np.outer(wave_z, cell % NZ), NZ) / NZ
    first = 2 * np.pi * turns + np.where(imag, np.pi / 2, 0.0)[:, None]
    tiles = NY * NZ // lanes
    step = 2 * np.pi * np.mod(np.outer(np.arange(tiles) * (lanes // NZ), wave_y), NY) / NY
    parts = [np.cos(first), np.sin(first), np.cos(step), np.sin(step)]
    cos0, sin0, cos_k, sin_k = lax.optimization_barrier(tuple(jnp.asarray(a, F32) for a in parts))
    return (cos0[None] * cos_k[:, :, None] - sin0[None] * sin_k[:, :, None]).astype(BF16)


def along_tables(devices):
    planes = NX // devices
    waves = np.arange(MX) - MX // 2
    angle = 2 * np.pi * np.mod(np.outer(waves, np.arange(NX)), NX) / NX
    cos = np.cos(angle).reshape(MX, devices, planes)
    sin = np.sin(angle).reshape(MX, devices, planes)
    to_real = np.stack([cos, sin], axis=2)
    to_imag = np.stack([-sin, cos], axis=2)
    forward = np.concatenate([to_real, to_imag], axis=0).reshape(2 * MX, 2 * NX)
    high = forward.astype(jnp.bfloat16).astype(np.float64)
    both = np.concatenate([high, forward - high], axis=0)
    return jnp.asarray(both, BF16), jnp.asarray(both.T, BF16)


def encode_kernel(devices, cap, owner, block, feat, kern, send, slot_of, targets, count):
    pairs = kern.shape[0]
    size = kern.shape[1]

    def clear(d, carry):
        count[d] = 0
        for i in range(cap):
            targets[d * cap + i] = -1
        send[d] = jnp.zeros(send.shape[1:], BF16)
        return carry

    lax.fori_loop(0, devices, clear, 0)

    def one(b, carry):
        values = feat[:, pl.ds(pl.multiple_of(b * size, size), size)]
        for k in range(NBR):
            p = b * NBR + k
            d = owner[p]
            n = count[d]
            count[d] = n + 1
            slot_of[p] = d * cap + n
            targets[d * cap + n] = block[p]
            rows = pl.ds(pl.multiple_of(n * values.shape[0], values.shape[0]), values.shape[0])
            send[d, rows, :] = jnp.dot(values, kern[p], preferred_element_type=F32).astype(BF16)
        return carry

    lax.fori_loop(0, pairs // NBR, one, 0)
    lane = lax.broadcasted_iota(jnp.int32, (NOTE_ROWS, size), 1)

    def note(d, carry):
        row = jnp.zeros((NOTE_ROWS, size), F32)
        for i in range(cap):
            row = jnp.where(lane == i, targets[d * cap + i].astype(F32), row)
        send[d, send.shape[1] - NOTE_ROWS :, :] = row.astype(BF16)
        return carry

    lax.fori_loop(0, devices, note, 0)


def table_tile(table, k, wide):
    return jnp.concatenate([table[k * wide + i] for i in range(wide)], axis=1)


def gather_sums_kernel(cap, channels, per_plane, wide, targets, got, table, field, spec, total):
    size = got.shape[2]
    chunk = wide * size
    tiles = table.shape[0] // wide

    def clear(k, carry):
        field[:, pl.ds(pl.multiple_of(k * chunk, chunk), chunk)] = jnp.zeros((field.shape[0], chunk), F32)
        return carry

    lax.fori_loop(0, tiles, clear, 0)

    def add(d, carry):
        for i in range(cap):
            t = targets[d * cap + i]

            @pl.when(t >= 0)
            def _():
                rows = pl.ds(pl.multiple_of(t // per_plane * channels, channels), channels)
                cols = pl.ds(pl.multiple_of(t % per_plane * size, size), size)
                field[rows, cols] += got[d, i * channels : (i + 1) * channels, :].astype(F32)

        return carry

    lax.fori_loop(0, got.shape[0], add, 0)
    total[...] = jnp.zeros_like(total)

    def transform(k, carry):
        values = field[:, pl.ds(pl.multiple_of(k * chunk, chunk), chunk)].astype(BF16)
        total[...] += lax.dot_general(table_tile(table, k, wide), values, NT, preferred_element_type=F32)
        return carry

    lax.fori_loop(0, tiles, transform, 0)
    spec[...] = total[...].astype(BF16)


def mix_kernel(channels, forward, inverse, data, weight, scaling, out, mixed):
    rows = 2 * MX
    here, fan = weight.shape[0], weight.shape[1] // (2 * channels)
    width = 2 * channels
    row_wave = lax.broadcasted_iota(jnp.int32, (rows, width), 0) % MX
    half = lax.broadcasted_iota(jnp.int32, (rows, width), 1) // channels
    left = half == 0
    modes = jnp.dot(forward[...], data[...], preferred_element_type=F32)
    modes = modes[:rows] + modes[rows:]
    for pair in range(here // 2):
        own = modes[:, pair * width : (pair + 1) * width]
        other = pltpu.roll(own, channels, 1)
        halves = []
        for k in range(2):
            twice = jnp.where(left, own, other) if k == 0 else jnp.where(left, other, own)
            spread = jnp.concatenate(
                [jnp.where(row_wave == 2 * f + half, twice, 0.0).astype(BF16) for f in range(fan)], axis=1
            )
            prod = jnp.dot(spread, weight[2 * pair + k], preferred_element_type=F32)
            real, imag = prod[:MX], prod[MX:]
            real_turned = pltpu.roll(real, channels, 1)
            imag_turned = pltpu.roll(imag, channels, 1)
            if k == 0:
                halves.append((real - imag_turned, real_turned + imag))
            else:
                halves.append((real_turned - imag, real + imag_turned))
        (real_a, imag_a), (real_b, imag_b) = halves
        top = left[:MX]
        both = jnp.concatenate([jnp.where(top, real_a, real_b), jnp.where(top, imag_a, imag_b)], axis=0)
        both = (both * scaling[:, pair * width : (pair + 1) * width]).astype(BF16)
        mixed[0:rows, pair * width : (pair + 1) * width] = both
        mixed[rows : 2 * rows, pair * width : (pair + 1) * width] = both
    out[...] = jnp.dot(inverse[...], mixed[...], preferred_element_type=F32).astype(BF16)


def layer_kernel(last, planes, wide, modes, table, field, up, down, out, *rest):
    channels = field.shape[0] // planes
    tile = table_tile(table, 0, wide)
    summed = out if not last else rest[0]
    summed[...] = field[...] + jnp.dot(modes[...], tile, preferred_element_type=F32)
    scale = math.sqrt(2.0 / math.pi)
    down_half = (down[...].astype(F32) * 0.5).astype(BF16)

    def raise_up(p):
        values = summed[p * channels : (p + 1) * channels, :]
        return jnp.dot(up[...], values.astype(BF16), preferred_element_type=F32).astype(BF16)

    ahead = raise_up(0)
    for p in range(planes):
        v = ahead
        if p + 1 < planes:
            ahead = raise_up(p + 1)
        rows = slice(p * channels, (p + 1) * channels)
        turn = jnp.tanh(v * (BF16(scale) + BF16(scale * 0.044715) * (v * v)))
        active = v + v * turn
        values = summed[rows, :] + jnp.dot(down_half, active, preferred_element_type=F32)
        out[rows, :] = values.astype(out.dtype)

    if not last:
        spec, total = rest

        @pl.when(pl.program_id(0) == 0)
        def _():
            total[...] = jnp.zeros_like(total)

        total[...] += lax.dot_general(tile, out[...].astype(BF16), NT, preferred_element_type=F32)

        @pl.when(pl.program_id(0) == pl.num_programs(0) - 1)
        def _():
            spec[...] = total[...].astype(BF16)


def pick_kernel(cap, per_plane, targets, field, send):
    channels, size = send.shape[2], send.shape[3]

    def one(d, carry):
        for i in range(cap):
            t = jnp.maximum(targets[d * cap + i], 0)
            rows = pl.ds(pl.multiple_of(t // per_plane * channels, channels), channels)
            cols = pl.ds(pl.multiple_of(t % per_plane * size, size), size)
            send[d, i] = field[rows, cols]
        return carry

    lax.fori_loop(0, send.shape[0], one, 0)


def decode_kernel(slot_of, got, kern, out):
    size = kern.shape[1]

    def one(b, carry):
        acc = None
        for k in range(NBR):
            p = b * NBR + k
            term = lax.dot_general(got[slot_of[p]], kern[p], NT, preferred_element_type=F32)
            acc = term if acc is None else acc + term
        out[:, pl.ds(pl.multiple_of(b * size, size), size)] = acc
        return carry

    lax.fori_loop(0, kern.shape[0] // NBR, one, 0)


def swap(values):
    return lax.all_to_all(values, "pen", split_axis=0, concat_axis=0, tiled=True)


def per_device(point_feat, pair_kernel, pair_owner, pair_block, spec_weight, mlp_up, mlp_down):
    devices = lax.axis_size("pen")
    pairs, size = pair_kernel.shape[0], pair_kernel.shape[1]
    channels = point_feat.shape[0]
    cap = 2 * pairs // devices
    planes = NX // devices
    plane_cells = NY * NZ
    per_plane = plane_cells // size
    here = spec_weight.shape[1]
    modes_all = MY * MZ
    hidden = mlp_up.shape[1]
    lines = planes * channels
    wide = 4
    table = plane_table(devices, size)
    forward, inverse = along_tables(devices)

    send, slot_of, targets = pl.pallas_call(
        functools.partial(encode_kernel, devices, cap),
        out_shape=(
            jax.ShapeDtypeStruct((devices, cap * channels + NOTE_ROWS, size), BF16),
            jax.ShapeDtypeStruct((pairs,), jnp.int32),
            jax.ShapeDtypeStruct((devices * cap,), jnp.int32),
        ),
        in_specs=[SMEM, SMEM, VMEM, VMEM],
        out_specs=(VMEM, SMEM, SMEM),
        scratch_shapes=[pltpu.SMEM((devices,), jnp.int32)],
        name="encode",
    )(pair_owner[:, 0], pair_block, point_feat, pair_kernel)
    got = swap(send)
    wanted = got[:, cap * channels, :cap].astype(jnp.int32).reshape(devices * cap)

    field, spec = pl.pallas_call(
        functools.partial(gather_sums_kernel, cap, channels, per_plane, wide),
        out_shape=(
            jax.ShapeDtypeStruct((lines, plane_cells), F32),
            jax.ShapeDtypeStruct((2 * modes_all, lines), BF16),
        ),
        in_specs=[SMEM, VMEM, VMEM],
        out_specs=(VMEM, VMEM),
        scratch_shapes=[pltpu.VMEM((2 * modes_all, lines), F32)],
        name="place",
    )(wanted, got, table)

    first_mode = lax.axis_index("pen") * here
    wave_z = (first_mode + jnp.arange(here * channels, dtype=jnp.int32) // channels) % MZ
    scaling = (jnp.where(wave_z == 0, 1.0, 2.0).astype(F32) / (NX * NY * NZ))[None, :]
    weights = spec_weight.reshape(LAYERS * here, MX * channels, 2 * channels)
    whole = lambda shape: pl.BlockSpec(shape, lambda g: (0,) * len(shape))
    for number in range(LAYERS):
        last = number == LAYERS - 1
        across = swap(spec.reshape(devices, 2 * here, lines))
        data = across.reshape(devices, 2, here, planes, channels).transpose(0, 1, 3, 2, 4)
        mixed = pl.pallas_call(
            functools.partial(mix_kernel, channels),
            out_shape=jax.ShapeDtypeStruct((2 * NX, here * channels), BF16),
            grid=(1,),
            in_specs=[
                whole((4 * MX, 2 * NX)),
                whole((2 * NX, 4 * MX)),
                whole((2 * NX, here * channels)),
                pl.BlockSpec((here, MX * channels, 2 * channels), lambda g, n=number: (n, 0, 0)),
                whole((1, here * channels)),
            ],
            out_specs=whole((2 * NX, here * channels)),
            scratch_shapes=[pltpu.VMEM((4 * MX, here * channels), BF16)],
            name="mix",
        )(forward, inverse, data.reshape(2 * NX, here * channels), weights, scaling)
        modes = swap(mixed.reshape(devices, 2 * planes, here * channels))
        modes = modes.reshape(devices, 2, planes, here, channels).transpose(0, 1, 3, 2, 4)
        modes = modes.reshape(2 * modes_all, lines).T

        chunk = wide * size
        spec_shape = (2 * modes_all, lines)
        field_spec = pl.BlockSpec((lines, chunk), lambda k: (0, k))
        results = pl.pallas_call(
            functools.partial(layer_kernel, last, planes, wide),
            out_shape=(jax.ShapeDtypeStruct((lines, plane_cells), BF16 if last else F32),)
            + (() if last else (jax.ShapeDtypeStruct(spec_shape, BF16),)),
            grid=(plane_cells // chunk,),
            in_specs=[
                pl.BlockSpec((lines, 2 * modes_all), lambda k: (0, 0)),
                pl.BlockSpec((wide, 2 * modes_all, size), lambda k: (k, 0, 0)),
                field_spec,
                pl.BlockSpec((hidden, channels), lambda k: (0, 0)),
                pl.BlockSpec((channels, hidden), lambda k: (0, 0)),
            ],
            out_specs=(field_spec,) + (() if last else (pl.BlockSpec(spec_shape, lambda k: (0, 0)),)),
            scratch_shapes=[pltpu.VMEM((lines, chunk) if last else spec_shape, F32)],
            name="layer",
        )(modes, table, field, mlp_up[number], mlp_down[number])
        if last:
            field = results[0]
        else:
            field, spec = results

    picked = pl.pallas_call(
        functools.partial(pick_kernel, cap, per_plane),
        out_shape=jax.ShapeDtypeStruct((devices, cap, channels, size), BF16),
        in_specs=[SMEM, VMEM],
        out_specs=VMEM,
        name="pick",
    )(wanted, field)
    fetched = swap(picked).reshape(devices * cap, channels, size)
    return pl.pallas_call(
        decode_kernel,
        out_shape=jax.ShapeDtypeStruct((channels, pairs // NBR * size), F32),
        in_specs=[SMEM, VMEM, VMEM],
        out_specs=VMEM,
        name="decode",
    )(slot_of, fetched, pair_kernel)


def solution(mesh):
    in_specs = (
        P(None, ("groups", "pen")),
        P(("groups", "pen"), None, None),
        P(("groups", "pen"), None),
        P(("groups", "pen")),
        P(None, "pen", None, None, None),
        P(),
        P(),
    )
    out_specs = P(None, ("groups", "pen"))
    return jax.shard_map(
        per_device, mesh=mesh, in_specs=in_specs, out_specs=out_specs, check_vma=False
    )
```

profile of v0, /device:TPU:17, one launch (start us, length us, event | category | flops | bytes accessed | tf_op | source)
XLA Modules:
  0.0 264.5 jit_solution(10909692110295504091)
XLA Ops:
  0.0 6.3 %encode.1 = (bf16[16,528,128]{2,1,0:T(8,128)(2,1)}, s32[64]{0:T(128)}, s32[128]{0:T(128)}) custom-call(s32[64]{0:T(128)} %bitcast.42, s32[64]{0:T(128)} %block.1, bf16[64,2048]{1,0:T(8,128)(2,1)} %feat.1, bf16[64,128,128]{2,1,0:T(8,128)(2,1)} %kern.3), custom_call_target="tpu_custom_call" | custom-call | tf_op jit(solution)/shard_map/encode/pallas_call | solution.py:259
  6.4 6.5 %all-to-all-start = ((bf16[16,528,128]{2,1,0:T(8,128)(2,1)}), bf16[16,528,128]{2,1,0:T(8,128)(2,1)S(1)}, u32[]{:S(2)}, u32[]{:S(2)}) async-start(bf16[16,528,128]{2,1,0:T(8,128)(2,1)} %get-tuple-element.16), calls=%async_computation | async-start | bytes 4325376 | tf_op jit(solution)/shard_map/all_to_all | solution.py:240
  12.8 7.7 %subtract_convert_fusion.table = bf16[32,512,128]{2,1,0:T(8,128)(2,1)} fusion(f32[32,512]{1,0:T(8,128)} %constant.59.clone, f32[512,128]{1,0:T(8,128)} %constant.57.clone, f32[32,512]{1,0:T(8,128)} %constant.58.clone, f32[512,128]{1,0:T(8,128)} %constant.56.clone), kind=kLoop, calls=%fused_computation | loop fusion | flops 8388608 | bytes 4849664 | tf_op jit(solution)/shard_map/convert_element_type | solution.py:43
  20.6 40.7 %all-to-all-done.got = bf16[16,528,128]{2,1,0:T(8,128)(2,1)S(1)} async-done(((bf16[16,528,128]{2,1,0:T(8,128)(2,1)}), bf16[16,528,128]{2,1,0:T(8,128)(2,1)S(1)}, u32[]{:S(2)}, u32[]{:S(2)}) %all-to-all-start) | async-done | bytes 2162720 | tf_op jit(solution)/shard_map/all_to_all | solution.py:240
  61.3 0.8 reshape.143.targets
  62.6 13.2 %place.1 = (f32[512,4096]{1,0:T(8,128)}, bf16[512,512]{1,0:T(8,128)(2,1)}) custom-call(s32[128]{0:T(128)} %reshape.143.targets, bf16[16,528,128]{2,1,0:T(8,128)(2,1)} %copy-done, bf16[32,512,128]{2,1,0:T(8,128)(2,1)} %subtract_convert_fusion.table), custom_call_target="tpu_custom_call" | custom-call | tf_op jit(solution)/shard_map/place/pallas_call | solution.py:274
  75.8 5.2 %all-to-all-start.1 = ((bf16[16,32,512]{2,1,0:T(8,128)(2,1)}), bf16[16,32,512]{2,1,0:T(8,128)(2,1)S(1)}, u32[]{:S(2)}, u32[]{:S(2)}) async-start(bf16[16,32,512]{2,1,0:T(8,128)(2,1)} %bitcast.38), calls=%async_computation.1 | async-start | bytes 1048576 | tf_op jit(solution)/shard_map/all_to_all | solution.py:240
  81.0 0.6 fusion.2.scaling
  81.6 12.5 %all-to-all-done.1 = bf16[16,32,512]{2,1,0:T(8,128)(2,1)S(1)} async-done(((bf16[16,32,512]{2,1,0:T(8,128)(2,1)}), bf16[16,32,512]{2,1,0:T(8,128)(2,1)S(1)}, u32[]{:S(2)}, u32[]{:S(2)}) %all-to-all-start.1) | async-done | bytes 524320 | tf_op jit(solution)/shard_map/all_to_all | solution.py:240
  94.9 1.5 reshape.131.data
  96.4 4.4 %mix.2 = bf16[256,1024]{1,0:T(8,128)(2,1)} custom-call(bf16[64,256]{1,0:T(8,128)(2,1)} %constant.60.clone.forward, bf16[256,64]{1,0:T(8,128)(2,1)} %constant.61.clone.inverse, bf16[256,1024]{1,0:T(8,128)(2,1)} %reshape.131.data, bf16[32,1024,128]{2,1,0:T(8,128)(2,1)} %bitcast.27, f32[1,1024]{1,0:T(1,128)} %fusion.2.scaling), custom_call_target="tpu_custom_call" | custom-call | tf_op jit(solution)/shard_map/mix/pallas_call | solution.py:295
  100.8 5.3 %all-to-all-start.2 = ((bf16[16,16,1024]{2,1,0:T(8,128)(2,1)}), bf16[16,16,1024]{2,1,0:T(8,128)(2,1)S(1)}, u32[]{:S(2)}, u32[]{:S(2)}) async-start(bf16[16,16,1024]{2,1,0:T(8,128)(2,1)} %bitcast.34), calls=%async_computation.2 | async-start | bytes 1048576 | tf_op jit(solution)/shard_map/all_to_all | solution.py:240
  106.1 0.7 copy.24
  106.9 0.6 slice_bitcast_fusion
  107.5 11.7 %all-to-all-done.2 = bf16[16,16,1024]{2,1,0:T(8,128)(2,1)S(1)} async-done(((bf16[16,16,1024]{2,1,0:T(8,128)(2,1)}), bf16[16,16,1024]{2,1,0:T(8,128)(2,1)S(1)}, u32[]{:S(2)}, u32[]{:S(2)}) %all-to-all-start.2) | async-done | bytes 524320 | tf_op jit(solution)/shard_map/all_to_all | solution.py:240
  119.2 0.7 reshape.134
  120.2 0.6 reshape.135
  120.8 1.0 copy.18
  121.8 18.8 %layer.2 = (f32[512,4096]{1,0:T(8,128)}, bf16[512,512]{1,0:T(8,128)(2,1)}) custom-call(bf16[512,512]{1,0:T(8,128)(2,1)} %bitcast.36, bf16[32,512,128]{2,1,0:T(8,128)(2,1)} %subtract_convert_fusion.table, f32[512,4096]{1,0:T(8,128)} %get-tuple-element.22.field, bf16[256,64]{1,0:T(8,128)(2,1)} %bitcast.40, bf16[64,256]{1,0:T(8,128)(2,1)} %get-tuple-element.26.down), custom_call_target="tpu_custom_call" | custom-call | tf_op jit(solution)/shard_map/layer/pallas_call | solution.py:317
  140.6 18.4 %all_to_all.30 = bf16[16,32,512]{2,1,0:T(8,128)(2,1)S(1)} all-to-all(bf16[16,32,512]{2,1,0:T(8,128)(2,1)} %bitcast.39), channel_id=1, replica_groups=mesh['groups'=2,'pen'=16] {'pen'}, dimensions={0} | all-to-all | bytes 1048576 | tf_op jit(solution)/shard_map/all_to_all | solution.py:240
  159.8 1.5 reshape.138.data
  161.4 4.4 %mix.3 = bf16[256,1024]{1,0:T(8,128)(2,1)} custom-call(bf16[64,256]{1,0:T(8,128)(2,1)} %constant.60.clone.forward, bf16[256,64]{1,0:T(8,128)(2,1)} %constant.61.clone.inverse, bf16[256,1024]{1,0:T(8,128)(2,1)} %reshape.138.data, bf16[32,1024,128]{2,1,0:T(8,128)(2,1)} %bitcast.28, f32[1,1024]{1,0:T(1,128)} %fusion.2.scaling), custom_call_target="tpu_custom_call" | custom-call | tf_op jit(solution)/shard_map/mix/pallas_call | solution.py:295
  165.8 5.3 %all-to-all-start.4 = ((bf16[16,16,1024]{2,1,0:T(8,128)(2,1)}), bf16[16,16,1024]{2,1,0:T(8,128)(2,1)S(1)}, u32[]{:S(2)}, u32[]{:S(2)}) async-start(bf16[16,16,1024]{2,1,0:T(8,128)(2,1)} %bitcast.35), calls=%async_computation.4 | async-start | bytes 1048576 | tf_op jit(solution)/shard_map/all_to_all | solution.py:240
  171.1 0.7 copy.25
  171.8 12.4 %all-to-all-done.4 = bf16[16,16,1024]{2,1,0:T(8,128)(2,1)S(1)} async-done(((bf16[16,16,1024]{2,1,0:T(8,128)(2,1)}), bf16[16,16,1024]{2,1,0:T(8,128)(2,1)S(1)}, u32[]{:S(2)}, u32[]{:S(2)}) %all-to-all-start.4) | async-done | bytes 524320 | tf_op jit(solution)/shard_map/all_to_all | solution.py:240
  184.2 0.7 reshape.140
  185.1 0.6 reshape.141
  185.8 1.0 copy.22
  186.8 14.8 %layer.3.field = bf16[512,4096]{1,0:T(8,128)(2,1)} custom-call(bf16[512,512]{1,0:T(8,128)(2,1)} %bitcast.37, bf16[32,512,128]{2,1,0:T(8,128)(2,1)} %subtract_convert_fusion.table, f32[512,4096]{1,0:T(8,128)} %get-tuple-element.24.field, bf16[256,64]{1,0:T(8,128)(2,1)} %bitcast.41, bf16[64,256]{1,0:T(8,128)(2,1)} %get-tuple-element.25.down), custom_call_target="tpu_custom_call" | custom-call | tf_op jit(solution)/shard_map/layer/pallas_call | solution.py:317
  201.5 4.3 %pick.1 = bf16[16,8,64,128]{3,2,1,0:T(8,128)(2,1)} custom-call(s32[128]{0:T(128)} %reshape.143.targets, bf16[512,4096]{1,0:T(8,128)(2,1)} %layer.3.field), custom_call_target="tpu_custom_call" | custom-call | tf_op jit(solution)/shard_map/pick/pallas_call | solution.py:338
  205.9 52.4 %all_to_all.31 = bf16[16,8,64,128]{3,2,1,0:T(8,128)(2,1)} all-to-all(bf16[16,8,64,128]{3,2,1,0:T(8,128)(2,1)} %pick.1), channel_id=1, replica_groups=mesh['groups'=2,'pen'=16] {'pen'}, dimensions={0} | all-to-all | bytes 4194304 | tf_op jit(solution)/shard_map/all_to_all | solution.py:240
  258.3 6.2 %decode.1 = f32[64,2048]{1,0:T(8,128)} custom-call(s32[64]{0:T(128)} %get-tuple-element.15.slot_of, bf16[128,64,128]{2,1,0:T(8,128)(2,1)} %bitcast.29, bf16[64,128,128]{2,1,0:T(8,128)(2,1)} %kern.3), custom_call_target="tpu_custom_call" | custom-call | tf_op jit(solution)/shard_map/decode/pallas_call | solution.py:346
  (14 shorter events, 2.6 us)
Async XLA Ops:
  6.4 54.9 %all-to-all-start = ((bf16[16,528,128]{2,1,0:T(8,128)(2,1)}), bf16[16,528,128]{2,1,0:T(8,128)(2,1)S(1)}, u32[]{:S(2)}, u32[]{:S(2)}) async-start(bf16[16,528,128]{2,1,0:T(8,128)(2,1)} %get-tuple-element.16), calls=%async_computation | async-start | bytes 4325376 | tf_op jit(solution)/shard_map/all_to_all | solution.py:240
  61.3 1.4 copy-start
  75.8 30.3 %copy-start.1 = (bf16[2,256,64]{1,2,0:T(8,128)(2,1)S(1)}, bf16[2,256,64]{1,2,0:T(8,128)(2,1)}, u32[]{:S(2)}) copy-start(bf16[2,256,64]{1,2,0:T(8,128)(2,1)} %param.18) | copy-start | bytes 196612
  75.8 31.0 %copy-start.2 = (bf16[2,64,256]{2,1,0:T(8,128)(2,1)S(1)}, bf16[2,64,256]{2,1,0:T(8,128)(2,1)}, u32[]{:S(2)}) copy-start(bf16[2,64,256]{2,1,0:T(8,128)(2,1)} %param.19) | copy-start | bytes 196612
  75.8 18.3 %all-to-all-start.1 = ((bf16[16,32,512]{2,1,0:T(8,128)(2,1)}), bf16[16,32,512]{2,1,0:T(8,128)(2,1)S(1)}, u32[]{:S(2)}, u32[]{:S(2)}) async-start(bf16[16,32,512]{2,1,0:T(8,128)(2,1)} %bitcast.38), calls=%async_computation.1 | async-start | bytes 1048576 | tf_op jit(solution)/shard_map/all_to_all | solution.py:240
  100.8 18.4 %all-to-all-start.2 = ((bf16[16,16,1024]{2,1,0:T(8,128)(2,1)}), bf16[16,16,1024]{2,1,0:T(8,128)(2,1)S(1)}, u32[]{:S(2)}, u32[]{:S(2)}) async-start(bf16[16,16,1024]{2,1,0:T(8,128)(2,1)} %bitcast.34), calls=%async_computation.2 | async-start | bytes 1048576 | tf_op jit(solution)/shard_map/all_to_all | solution.py:240
  165.8 18.4 %all-to-all-start.4 = ((bf16[16,16,1024]{2,1,0:T(8,128)(2,1)}), bf16[16,16,1024]{2,1,0:T(8,128)(2,1)S(1)}, u32[]{:S(2)}, u32[]{:S(2)}) async-start(bf16[16,16,1024]{2,1,0:T(8,128)(2,1)} %bitcast.35), calls=%async_computation.4 | async-start | bytes 1048576 | tf_op jit(solution)/shard_map/all_to_all | solution.py:240
where the time goes:
time: 268 us; the launch traced here: 264 us
  waiting for transfers between devices  77.3 us (29%)
  Pallas kernels  72.4 us (27%)
  blocking collectives  70.8 us (26%)
  starting transfers between devices  22.3 us (8%)
  local copies, waits for them, and re-layouts  13.1 us (5%)
  other arithmetic  8.39 us (3%)
    all_to_all x4, waiting for transfers between devices, swap(): lax.all_to_all(values, 'pen', split_axis=0, concat_axis=0, tiled=True)  77.3 us
    all_to_all x2, blocking collectives, swap(): lax.all_to_all(values, 'pen', split_axis=0, concat_axis=0, tiled=True)  70.8 us
    pallas_call x2, Pallas kernels, per_device(): pl.pallas_call(functools.partial(layer_kernel, last, planes, wide), out_s...  33.6 us
    all_to_all x4, starting transfers between devices, swap(): lax.all_to_all(values, 'pen', split_axis=0, concat_axis=0, tiled=True)  22.3 us
    pallas_call x1, Pallas kernels, per_device(): pl.pallas_call(functools.partial(gather_sums_kernel, cap, channels, per_p...  13.2 us
    pallas_call x2, Pallas kernels, per_device(): pl.pallas_call(functools.partial(mix_kernel, channels), out_shape=jax.Sha...  8.74 us
    convert_element_type x1, other arithmetic, plane_table(): (cos0[None] * cos_k[:, :, None] - sin0[None] * sin_k[:, :, None]).astype(...  7.74 us
    pallas_call x1, Pallas kernels, per_device(): pl.pallas_call(functools.partial(encode_kernel, devices, cap), out_shape=...  6.35 us
  transfers between devices with their start and end apart: 4, of which 4 were waited for; matrix products, arithmetic and copies ran while one was open for 4% of the time, Pallas kernels for 0%

commit v1 on v0

--- a/solution.py
+++ b/solution.py
@@ -24,6 +24,9 @@
 VMEM = pl.BlockSpec(memory_space=pltpu.VMEM)
 SMEM = pl.BlockSpec(memory_space=pltpu.SMEM)
 NT = (((1,), (1,)), ((), ()))
+TN = (((0,), (0,)), ((), ()))
+MESH = pl.DeviceIdType.MESH
+ANY = pl.BlockSpec(memory_space=pl.ANY)
 
 
 def plane_table(devices, lanes):
@@ -54,7 +57,8 @@
     forward = np.concatenate([to_real, to_imag], axis=0).reshape(2 * MX, 2 * NX)
     high = forward.astype(jnp.bfloat16).astype(np.float64)
     both = np.concatenate([high, forward - high], axis=0)
-    return jnp.asarray(both, BF16), jnp.asarray(both.T, BF16)
+    own = jnp.asarray(forward.reshape(2 * MX, devices, 2 * planes).transpose(1, 2, 0), BF16)
+    return jnp.asarray(both, BF16), own
 
 
 def encode_kernel(devices, cap, owner, block, feat, kern, send, slot_of, targets, count):
@@ -100,7 +104,7 @@
     return jnp.concatenate([table[k * wide + i] for i in range(wide)], axis=1)
 
 
-def gather_sums_kernel(cap, channels, per_plane, wide, targets, got, table, field, spec, total):
+def gather_sums_kernel(cap, channels, per_plane, wide, targets, got, table, field, spec, send, total):
     size = got.shape[2]
     chunk = wide * size
     tiles = table.shape[0] // wide
@@ -124,6 +128,16 @@
         return carry
 
     lax.fori_loop(0, got.shape[0], add, 0)
+
+    def pick(d, carry):
+        for i in range(cap):
+            t = jnp.maximum(targets[d * cap + i], 0)
+            rows = pl.ds(pl.multiple_of(t // per_plane * channels, channels), channels)
+            cols = pl.ds(pl.multiple_of(t % per_plane * size, size), size)
+            send[d, i] = field[rows, cols].astype(BF16)
+        return carry
+
+    lax.fori_loop(0, got.shape[0], pick, 0)
     total[...] = jnp.zeros_like(total)
 
     def transform(k, carry):
@@ -135,15 +149,93 @@
     spec[...] = total[...].astype(BF16)
 
 
-def mix_kernel(channels, forward, inverse, data, weight, scaling, out, mixed):
+def pen_position(me):
+    return me // 4, me // 2 % 2, me % 2
+
+
+def greet(partners):
+    barrier = pltpu.get_barrier_semaphore()
+    for d in partners:
+        pl.semaphore_signal(barrier, inc=1, device_id={"pen": d}, device_id_type=MESH)
+    pl.semaphore_wait(barrier, len(partners))
+
+
+def quad_partners(me, depth):
+    z, y, c = pen_position(me)
+    line = [(z + s) % depth * 4 + y * 2 + c for s in range(1, depth)]
+    return line, me + 2 - 4 * y, me + 1 - 2 * c
+
+
+def gather_blocks(me, depth, full, z_send, z_recv, y_send, y_recv, c_send, c_recv, arrived):
+    z, y, c = pen_position(me)
+    line, side, twin = quad_partners(me, depth)
+    started = []
+
+    def push(block, target, send_sem, recv_sem):
+        copy = pltpu.make_async_remote_copy(
+            src_ref=full.at[block],
+            dst_ref=full.at[block],
+            send_sem=send_sem,
+            recv_sem=recv_sem,
+            device_id={"pen": target},
+            device_id_type=MESH,
+        )
+        copy.start()
+        started.append(copy)
+
+    def landed(block, send_sem, recv_sem):
+        pltpu.make_async_remote_copy(
+            src_ref=full.at[block],
+            dst_ref=full.at[block],
+            send_sem=send_sem,
+            recv_sem=recv_sem,
+            device_id={"pen": twin},
+            device_id_type=MESH,
+        ).wait_recv()
+
+    for s in range(1, depth):
+        push(me, line[s - 1], z_send.at[s - 1], z_recv.at[s - 1])
+    push(me, side, y_send.at[0], y_recv.at[0])
+    push(me, twin, c_send.at[0], c_recv.at[0])
+    arrived(me)
+    for s in range(1, depth):
+        block = (z + depth - s) % depth * 4 + y * 2 + c
+        landed(block, z_send.at[s - 1], z_recv.at[s - 1])
+        push(block, side, y_send.at[s], y_recv.at[s])
+        push(block, twin, c_send.at[s], c_recv.at[s])
+        arrived(block)
+    for s in range(depth):
+        block = (z + depth - s) % depth * 4 + (1 - y) * 2 + c
+        landed(block, y_send.at[s], y_recv.at[s])
+        push(block, twin, c_send.at[depth + s], c_recv.at[depth + s])
+        arrived(block)
+    for s in range(depth):
+        block = (z + depth - s) % depth * 4 + y * 2 + 1 - c
+        landed(block, c_send.at[s], c_recv.at[s])
+        arrived(block)
+    for s in range(depth):
+        block = (z + depth - s) % depth * 4 + (1 - y) * 2 + 1 - c
+        landed(block, c_send.at[depth + s], c_recv.at[depth + s])
+        arrived(block)
+    for copy in started:
+        copy.wait_send()
+
+
+def mix_kernel(number, channels, planes, depth, forward, inverse, data, weights, scaling, full, spread_out, weight, fetch_sem, *sems):
     rows = 2 * MX
     here, fan = weight.shape[0], weight.shape[1] // (2 * channels)
+    me = lax.axis_index("pen")
+    line, side, twin = quad_partners(me, depth)
+    fetch = pltpu.make_async_copy(weights.at[pl.ds(number * here, here)], weight, fetch_sem)
+    fetch.start()
+    greet(line + [side, twin])
     width = 2 * channels
     row_wave = lax.broadcasted_iota(jnp.int32, (rows, width), 0) % MX
     half = lax.broadcasted_iota(jnp.int32, (rows, width), 1) // channels
     left = half == 0
     modes = jnp.dot(forward[...], data[...], preferred_element_type=F32)
     modes = modes[:rows] + modes[rows:]
+    fetch.wait()
     for pair in range(here // 2):
         own = modes[:, pair * width : (pair + 1) * width]
         other = pltpu.roll(own, channels, 1)
@@ -165,17 +257,47 @@
         top = left[:MX]
         both = jnp.concatenate([jnp.where(top, real_a, real_b), jnp.where(top, imag_a, imag_b)], axis=0)
         both = (both * scaling[:, pair * width : (pair + 1) * width]).astype(BF16)
-        mixed[0:rows, pair * width : (pair + 1) * width] = both
-        mixed[rows : 2 * rows, pair * width : (pair + 1) * width] = both
-    out[...] = jnp.dot(inverse[...], mixed[...], preferred_element_type=F32).astype(BF16)
-
-
-def layer_kernel(last, planes, wide, modes, table, field, up, down, out, *rest):
+        full[me, :, pair * width : (pair + 1) * width] = both
+
+    def arrived(block):
+        spread_out[block] = jnp.dot(inverse[0], full[block], preferred_element_type=F32).astype(BF16)
+
+    gather_blocks(me, depth, full, *sems, arrived)
+
+
+def gelu_twice(v):
+    scale = math.sqrt(2.0 / math.pi)
+    turn = jnp.tanh(v * (BF16(scale) + BF16(scale * 0.044715) * (v * v)))
+    return v + v * turn
+
+
+def layer_kernel(devices, planes, wide, modes, table, field, up, down, picked, spec, fetched, total, summed, out, own_sem, send_sem, recv_sem):
     channels = field.shape[0] // planes
+    me = lax.axis_index("pen")
+    step, steps = pl.program_id(0), pl.num_programs(0)
+
+    def exchange(j):
+        return pltpu.make_async_remote_copy(
+            src_ref=picked.at[(me + j) % devices],
+            dst_ref=fetched.at[me],
+            send_sem=send_sem.at[j],
+            recv_sem=recv_sem.at[j],
+            device_id={"pen": (me + j) % devices},
+            device_id_type=MESH,
+        )
+
+    own = pltpu.make_async_copy(picked.at[me], fetched.at[me], own_sem)
+
+    @pl.when(step == 0)
+    def _():
+        total[...] = jnp.zeros_like(total)
+        greet([(me + j) % devices for j in range(1, devices)])
+        own.start()
+        for j in range(1, devices):
+            exchange(j).start()
+
     tile = table_tile(table, 0, wide)
-    summed = out if not last else rest[0]
     summed[...] = field[...] + jnp.dot(modes[...], tile, preferred_element_type=F32)
-    scale = math.sqrt(2.0 / math.pi)
     down_half = (down[...].astype(F32) * 0.5).astype(BF16)
 
     def raise_up(p):
@@ -188,52 +310,93 @@
         if p + 1 < planes:
             ahead = raise_up(p + 1)
         rows = slice(p * channels, (p + 1) * channels)
-        turn = jnp.tanh(v * (BF16(scale) + BF16(scale * 0.044715) * (v * v)))
-        active = v + v * turn
-        values = summed[rows, :] + jnp.dot(down_half, active, preferred_element_type=F32)
-        out[rows, :] = values.astype(out.dtype)
-
-    if not last:
-        spec, total = rest
-
-        @pl.when(pl.program_id(0) == 0)
-        def _():
-            total[...] = jnp.zeros_like(total)
-
-        total[...] += lax.dot_general(tile, out[...].astype(BF16), NT, preferred_element_type=F32)
-
-        @pl.when(pl.program_id(0) == pl.num_programs(0) - 1)
-        def _():
-            spec[...] = total[...].astype(BF16)
-
-
-def pick_kernel(cap, per_plane, targets, field, send):
-    channels, size = send.shape[2], send.shape[3]
-
-    def one(d, carry):
-        for i in range(cap):
-            t = jnp.maximum(targets[d * cap + i], 0)
-            rows = pl.ds(pl.multiple_of(t // per_plane * channels, channels), channels)
-            cols = pl.ds(pl.multiple_of(t % per_plane * size, size), size)
-            send[d, i] = field[rows, cols]
-        return carry
-
-    lax.fori_loop(0, send.shape[0], one, 0)
-
-
-def decode_kernel(slot_of, got, kern, out):
+        values = summed[rows, :] + jnp.dot(down_half, gelu_twice(v), preferred_element_type=F32)
+        out[rows, :] = values.astype(BF16)
+    total[...] += lax.dot_general(tile, out[...], NT, preferred_element_type=F32)
+
+    @pl.when(step == steps - 1)
+    def _():
+        spec[...] = total[...].astype(BF16)
+        own.wait()
+        for j in range(1, devices):
+            exchange(j).wait_send()
+        for j in range(1, devices):
+            pltpu.make_async_remote_copy(
+                src_ref=picked.at[me],
+                dst_ref=fetched.at[(me + devices - j) % devices],
+                send_sem=send_sem.at[j],
+                recv_sem=recv_sem.at[j],
+                device_id={"pen": (me + devices - j) % devices},
+                device_id_type=MESH,
+            ).wait_recv()
+
+
+def point_phases(owner, block, planes, per_plane, lines_here):
+    x = owner * planes + block // per_plane
+    y = (block % per_plane)[None, :] * lines_here + jnp.arange(lines_here, dtype=jnp.int32)[:, None]
+    wave_x = jnp.arange(MX, dtype=jnp.int32) - MX // 2
+    wave_y = jnp.arange(MY, dtype=jnp.int32) - MY // 2
+    turns_x = jnp.mod(x[:, None] * wave_x[None, :], NX).astype(F32) / NX
+    turns_y = jnp.mod(y[:, :, None] * wave_y[None, None, :], NY).astype(F32) / NY
+    angle = 2 * math.pi * (turns_x[None, :, None, :] + turns_y[:, :, :, None])
+    cos, sin = jnp.cos(angle), jnp.sin(angle)
+    real = jnp.stack([cos, -sin], axis=3)
+    imag = jnp.stack([sin, cos], axis=3)
+    rows = 2 * lines_here * x.shape[0]
+    return jnp.stack([real, imag], axis=0).reshape(rows, MY * 2 * MX).astype(BF16)
+
+
+def depth_table(size):
+    lines_here = size // NZ
+    wave = np.arange(MZ)
+    cell = np.arange(size)
+    angle = 2 * np.pi * np.mod(np.outer(wave, cell % NZ), NZ) / NZ
+    on_line = (cell // NZ)[None, :] == np.arange(lines_here)[:, None]
+    parts = np.stack([np.cos(angle), -np.sin(angle)], axis=1)
+    full = parts[:, :, None, :] * on_line[None, None, :, :]
+    full = full.reshape(MZ // 2, 2, 2 * lines_here, size).transpose(0, 2, 1, 3)
+    return jnp.asarray(full.reshape(MZ // 2 * 2 * lines_here, 2 * size), BF16)
+
+
+def answer_kernel(channels, group, slot_of, got, kern, phases, first, second, depths, up, down, out, waves):
     size = kern.shape[1]
-
-    def one(b, carry):
-        acc = None
-        for k in range(NBR):
-            p = b * NBR + k
-            term = lax.dot_general(got[slot_of[p]], kern[p], NT, preferred_element_type=F32)
-            acc = term if acc is None else acc + term
-        out[:, pl.ds(pl.multiple_of(b * size, size), size)] = acc
-        return carry
-
-    lax.fori_loop(0, kern.shape[0] // NBR, one, 0)
+    pairs = kern.shape[0]
+    tall = phases.shape[0]
+    lane = 2 * channels
+    per_group = first.shape[2] // lane
+    for number, full in enumerate((first, second)):
+        for g in range(full.shape[0]):
+            for w in range(per_group):
+                part = jnp.dot(phases[...], full[g, :, w * lane : (w + 1) * lane], preferred_element_type=F32)
+                start = (g * per_group + w) * tall
+                waves[number, start : start + tall, :] = part
+    count = waves.shape[1] // pairs
+
+    def spectral(number, p):
+        value = waves[number, pl.ds(p, count, stride=pairs), :].astype(BF16)
+        wide = lax.dot_general(value, depths[...], TN, preferred_element_type=F32)
+        return wide[:channels, :size] + wide[channels:, size:]
+
+    downs = [(down[n].astype(F32) * 0.5).astype(BF16) for n in range(LAYERS)]
+
+    def body(b, carry):
+        todo = [(b * group + i) * NBR + k for i in range(group) for k in range(NBR)]
+        values = jnp.concatenate([got[slot_of[p]].astype(F32) for p in todo], axis=1)
+        for n in range(LAYERS):
+            summed = values + jnp.concatenate([spectral(n, p) for p in todo], axis=1)
+            v = jnp.dot(up[n], summed.astype(BF16), preferred_element_type=F32).astype(BF16)
+            values = summed + jnp.dot(downs[n], gelu_twice(v), preferred_element_type=F32)
+        values = values.astype(BF16)
+        for i in range(group):
+            acc = None
+            for k in range(NBR):
+                at = (i * NBR + k) * size
+                term = lax.dot_general(values[:, at : at + size], kern[todo[i * NBR + k]], NT, preferred_element_type=F32)
+                acc = term if acc is None else acc + term
+            out[:, pl.ds(pl.multiple_of((b * group + i) * size, size), size)] = acc
+        return carry
+
+    lax.fori_loop(0, pairs // NBR // group, body, 0)
 
 
 def swap(values):
@@ -271,85 +434,97 @@
     got = swap(send)
     wanted = got[:, cap * channels, :cap].astype(jnp.int32).reshape(devices * cap)
 
-    field, spec = pl.pallas_call(
+    field, spec, picked = pl.pallas_call(
         functools.partial(gather_sums_kernel, cap, channels, per_plane, wide),
         out_shape=(
             jax.ShapeDtypeStruct((lines, plane_cells), F32),
             jax.ShapeDtypeStruct((2 * modes_all, lines), BF16),
+            jax.ShapeDtypeStruct((devices, cap, channels, size), BF16),
         ),
         in_specs=[SMEM, VMEM, VMEM],
-        out_specs=(VMEM, VMEM),
+        out_specs=(VMEM, VMEM, VMEM),
         scratch_shapes=[pltpu.VMEM((2 * modes_all, lines), F32)],
         name="place",
     )(wanted, got, table)
 
-    first_mode = lax.axis_index("pen") * here
-    wave_z = (first_mode + jnp.arange(here * channels, dtype=jnp.int32) // channels) % MZ
+    me = lax.axis_index("pen")
+    depth = devices // 4
+    wave_z = (me * here + jnp.arange(here * channels, dtype=jnp.int32) // channels) % MZ
     scaling = (jnp.where(wave_z == 0, 1.0, 2.0).astype(F32) / (NX * NY * NZ))[None, :]
     weights = spec_weight.reshape(LAYERS * here, MX * channels, 2 * channels)
-    whole = lambda shape: pl.BlockSpec(shape, lambda g: (0,) * len(shape))
+    own_inverse = lax.dynamic_slice_in_dim(inverse, me, 1, axis=0)
+    lines_here = size // NZ
+    phases = point_phases(pair_owner[:, 0], pair_block, planes, per_plane, lines_here)
+    fulls = []
     for number in range(LAYERS):
         last = number == LAYERS - 1
         across = swap(spec.reshape(devices, 2 * here, lines))
         data = across.reshape(devices, 2, here, planes, channels).transpose(0, 1, 3, 2, 4)
-        mixed = pl.pallas_call(
-            functools.partial(mix_kernel, channels),
-            out_shape=jax.ShapeDtypeStruct((2 * NX, here * channels), BF16),
-            grid=(1,),
-            in_specs=[
-                whole((4 * MX, 2 * NX)),
-                whole((2 * NX, 4 * MX)),
-                whole((2 * NX, here * channels)),
-                pl.BlockSpec((here, MX * channels, 2 * channels), lambda g, n=number: (n, 0, 0)),
-                whole((1, here * channels)),
+        full, modes = pl.pallas_call(
+            functools.partial(mix_kernel, number, channels, planes, depth),
+            out_shape=(
+                jax.ShapeDtypeStruct((devices, 2 * MX, here * channels), BF16),
+                jax.ShapeDtypeStruct((devices, 2 * planes, here * channels), BF16),
+            ),
+            in_specs=[VMEM, VMEM, VMEM, ANY, VMEM],
+            out_specs=(VMEM, VMEM),
+            scratch_shapes=[
+                pltpu.VMEM((here, MX * channels, 2 * channels), BF16),
+                pltpu.SemaphoreType.DMA,
+                pltpu.SemaphoreType.DMA((depth - 1,)),
+                pltpu.SemaphoreType.DMA((depth - 1,)),
+                pltpu.SemaphoreType.DMA((depth,)),
+                pltpu.SemaphoreType.DMA((depth,)),
+                pltpu.SemaphoreType.DMA((2 * depth,)),
+                pltpu.SemaphoreType.DMA((2 * depth,)),
             ],
-            out_specs=whole((2 * NX, here * channels)),
-            scratch_shapes=[pltpu.VMEM((4 * MX, here * channels), BF16)],
+            compiler_params=pltpu.CompilerParams(collective_id=number, has_side_effects=True),
             name="mix",
-        )(forward, inverse, data.reshape(2 * NX, here * channels), weights, scaling)
-        modes = swap(mixed.reshape(devices, 2 * planes, here * channels))
+        )(forward, own_inverse, data.reshape(2 * NX, here * channels), weights, scaling)
+        fulls.append(full.reshape(MY, MZ // here, 2 * MX, here * channels).transpose(1, 0, 2, 3).reshape(MZ // here, MY * 2 * MX, here * channels))
+        if last:
+            break
         modes = modes.reshape(devices, 2, planes, here, channels).transpose(0, 1, 3, 2, 4)
         modes = modes.reshape(2 * modes_all, lines).T
 
         chunk = wide * size
         spec_shape = (2 * modes_all, lines)
-        field_spec = pl.BlockSpec((lines, chunk), lambda k: (0, k))
-        results = pl.pallas_call(
-            functools.partial(layer_kernel, last, planes, wide),
-            out_shape=(jax.ShapeDtypeStruct((lines, plane_cells), BF16 if last else F32),)
-            + (() if last else (jax.ShapeDtypeStruct(spec_shape, BF16),)),
+        spec, fetched = pl.pallas_call(
+            functools.partial(layer_kernel, devices, planes, wide),
+            out_shape=(
+                jax.ShapeDtypeStruct(spec_shape, BF16),
+                jax.ShapeDtypeStruct((devices, cap, channels, size), BF16),
+            ),
             grid=(plane_cells // chunk,),
             in_specs=[
                 pl.BlockSpec((lines, 2 * modes_all), lambda k: (0, 0)),
                 pl.BlockSpec((wide, 2 * modes_all, size), lambda k: (k, 0, 0)),
-                field_spec,
+                pl.BlockSpec((lines, chunk), lambda k: (0, k)),
                 pl.BlockSpec((hidden, channels), lambda k: (0, 0)),
                 pl.BlockSpec((channels, hidden), lambda k: (0, 0)),
+                ANY,
             ],
-            out_specs=(field_spec,) + (() if last else (pl.BlockSpec(spec_shape, lambda k: (0, 0)),)),
-            scratch_shapes=[pltpu.VMEM((lines, chunk) if last else spec_shape, F32)],
+            out_specs=(pl.BlockSpec(spec_shape, lambda k: (0, 0)), ANY),
+            scratch_shapes=[
+                pltpu.VMEM(spec_shape, F32),
+                pltpu.VMEM((lines, chunk), F32),
+                pltpu.VMEM((lines, chunk), BF16),
+                pltpu.SemaphoreType.DMA,
+                pltpu.SemaphoreType.DMA((devices,)),
+                pltpu.SemaphoreType.DMA((devices,)),
+            ],
+            compiler_params=pltpu.CompilerParams(collective_id=LAYERS + number, has_side_effects=True),
             name="layer",
-        )(modes, table, field, mlp_up[number], mlp_down[number])
-        if last:
-            field = results[0]
-        else:
-            field, spec = results
-
-    picked = pl.pallas_call(
-        functools.partial(pick_kernel, cap, per_plane),
-        out_shape=jax.ShapeDtypeStruct((devices, cap, channels, size), BF16),
-        in_specs=[SMEM, VMEM],
+        )(modes, table, field, mlp_up[number], mlp_down[number], picked)
+
+    return pl.pallas_call(
+        functools.partial(answer_kernel, channels, 2),
+        out_shape=jax.ShapeDtypeStruct((channels, pairs // NBR * size), F32),
+        in_specs=[SMEM] + [VMEM] * 8,
         out_specs=VMEM,
-        name="pick",
-    )(wanted, field)
-    fetched = swap(picked).reshape(devices * cap, channels, size)
-    return pl.pallas_call(
-        decode_kernel,
-        out_shape=jax.ShapeDtypeStruct((channels, pairs // NBR * size), F32),
-        in_specs=[SMEM, VMEM, VMEM],
-        out_specs=VMEM,
-        name="decode",
-    )(slot_of, fetched, pair_kernel)
+        scratch_shapes=[pltpu.VMEM((LAYERS, MZ // 2 * 2 * lines_here * pairs, 2 * channels), F32)],
+        name="answer",
+    )(slot_of, fetched.reshape(devices * cap, channels, size), pair_kernel, phases, *fulls, depth_table(size), mlp_up, mlp_down)
 
 
 def solution(mesh):

time: 268 us -> 231 us (0.86)
  blocking collectives: 70.8 us -> 0 us
  Pallas kernels: 72.4 us -> 125 us
  waiting for transfers between devices: 77.3 us -> 59.6 us
  starting transfers between devices: 22.3 us -> 19.5 us
    all_to_all x2 -> x0, blocking collectives: 70.8 us -> none  [swap(): lax.all_to_all(values, 'pen', split_axis=0, concat_axis=0, tiled=True)]
    pallas_call x6 -> x4, Pallas kernels: 52.9 us -> 105 us  [the longest x1 51.5 us: per_device(): pl.pallas_call(functools.partial(layer_kernel, devices, planes, wide), ou...]
    all_to_all x4 -> x3, waiting for transfers between devices: 77.3 us -> 59.6 us  [swap(): lax.all_to_all(values, 'pen', split_axis=0, concat_axis=0, tiled=True)]
    all_to_all x4 -> x3, starting transfers between devices: 22.3 us -> 19.5 us  [swap(): lax.all_to_all(values, 'pen', split_axis=0, concat_axis=0, tiled=True)]
  transfers between devices with their start and end apart: 4 -> 3, of which waited for: 4 -> 3; matrix products, arithmetic and copies ran while one was open for 4% -> 7% of each run, Pallas kernels for 0% -> 0%
where the time goes in v1:
time: 231 us; the launch traced here: 229 us
  Pallas kernels  125 us (54%)
  waiting for transfers between devices  59.6 us (26%)
  starting transfers between devices  19.5 us (8%)
  local copies, waits for them, and re-layouts  14.8 us (6%)
  other arithmetic  9.8 us (4%)
    all_to_all x3, waiting for transfers between devices, swap(): lax.all_to_all(values, 'pen', split_axis=0, concat_axis=0, tiled=True)  59.6 us
    pallas_call x1, Pallas kernels, per_device(): pl.pallas_call(functools.partial(layer_kernel, devices, planes, wide), ou...  51.5 us
    pallas_call x2, Pallas kernels, per_device(): pl.pallas_call(functools.partial(mix_kernel, number, channels, planes, de...  36.9 us
    all_to_all x3, starting transfers between devices, swap(): lax.all_to_all(values, 'pen', split_axis=0, concat_axis=0, tiled=True)  19.5 us
    pallas_call x1, Pallas kernels, per_device(): pl.pallas_call(functools.partial(answer_kernel, channels, 2), out_shape=j...  16.2 us
    pallas_call x1, Pallas kernels, per_device(): pl.pallas_call(functools.partial(gather_sums_kernel, cap, channels, per_p...  13.7 us
    convert_element_type x1, other arithmetic, plane_table(): (cos0[None] * cos_k[:, :, None] - sin0[None] * sin_k[:, :, None]).astype(...  7.71 us
    pallas_call x1, Pallas kernels, per_device(): pl.pallas_call(functools.partial(encode_kernel, devices, cap), out_shape=...  6.34 us
  transfers between devices with their start and end apart: 3, of which 3 were waited for; matrix products, arithmetic and copies ran while one was open for 7% of the time, Pallas kernels for 0%

profile of v1, /device:TPU:17, one launch (start us, length us, event | category | flops | bytes accessed | tf_op | source)
XLA Modules:
  0.0 228.5 jit_solution(17775660474605002403)
XLA Ops:
  0.0 6.3 %encode.1 = (bf16[16,528,128]{2,1,0:T(8,128)(2,1)}, s32[64]{0:T(128)}, s32[128]{0:T(128)}) custom-call(s32[64]{0:T(128)} %bitcast.41, s32[64]{0:T(128)} %block.1, bf16[64,2048]{1,0:T(8,128)(2,1)} %feat.1, bf16[64,128,128]{2,1,0:T(8,128)(2,1)} %kern.3), custom_call_target="tpu_custom_call" | custom-call | tf_op jit(solution)/shard_map/encode/pallas_call | solution.py:422
  6.4 6.6 %all-to-all-start = ((bf16[16,528,128]{2,1,0:T(8,128)(2,1)}), bf16[16,528,128]{2,1,0:T(8,128)(2,1)S(1)}, u32[]{:S(2)}, u32[]{:S(2)}) async-start(bf16[16,528,128]{2,1,0:T(8,128)(2,1)} %get-tuple-element.20), calls=%async_computation | async-start | bytes 4325376 | tf_op jit(solution)/shard_map/all_to_all | solution.py:403
  13.0 1.0 copy.29.up
  14.0 0.6 fusion.10.scaling
  14.6 7.7 %subtract_convert_fusion.table = bf16[32,512,128]{2,1,0:T(8,128)(2,1)} fusion(f32[32,512]{1,0:T(8,128)} %constant.128.clone, f32[512,128]{1,0:T(8,128)} %constant.126.clone, f32[32,512]{1,0:T(8,128)} %constant.127.clone, f32[512,128]{1,0:T(8,128)} %constant.125.clone), kind=kLoop, calls=%fused_computation | loop fusion | flops 8388608 | bytes 4849664 | tf_op jit(solution)/shard_map/convert_element_type | solution.py:46
  22.3 39.1 %all-to-all-done.got = bf16[16,528,128]{2,1,0:T(8,128)(2,1)S(1)} async-done(((bf16[16,528,128]{2,1,0:T(8,128)(2,1)}), bf16[16,528,128]{2,1,0:T(8,128)(2,1)S(1)}, u32[]{:S(2)}, u32[]{:S(2)}) %all-to-all-start) | async-done | bytes 2162720 | tf_op jit(solution)/shard_map/all_to_all | solution.py:403
  61.5 0.7 reshape.224.targets
  62.2 0.6 copy-done
  62.8 13.7 %place.1 = (f32[512,4096]{1,0:T(8,128)}, bf16[512,512]{1,0:T(8,128)(2,1)}, bf16[16,8,64,128]{3,2,1,0:T(8,128)(2,1)}) custom-call(s32[128]{0:T(128)} %reshape.224.targets, bf16[16,528,128]{2,1,0:T(8,128)(2,1)} %copy-done, bf16[32,512,128]{2,1,0:T(8,128)(2,1)} %subtract_convert_fusion.table), custom_call_target="tpu_custom_call" | custom-call | tf_op jit(solution)/shard_map/place/pallas_call | solution.py:437
  76.5 5.5 %all-to-all-start.1 = ((bf16[16,32,512]{2,1,0:T(8,128)(2,1)}), bf16[16,32,512]{2,1,0:T(8,128)(2,1)S(1)}, u32[]{:S(2)}, u32[]{:S(2)}) async-start(bf16[16,32,512]{2,1,0:T(8,128)(2,1)} %bitcast.40), calls=%async_computation.1 | async-start | bytes 1048576 | tf_op jit(solution)/shard_map/all_to_all | solution.py:403
  82.0 1.3 constant_dynamic-slice_fusion.inverse
  83.3 0.6 slice_bitcast_fusion.1.down
  83.9 0.6 slice_bitcast_fusion.up
  84.5 10.6 %all-to-all-done.1 = bf16[16,32,512]{2,1,0:T(8,128)(2,1)S(1)} async-done(((bf16[16,32,512]{2,1,0:T(8,128)(2,1)}), bf16[16,32,512]{2,1,0:T(8,128)(2,1)S(1)}, u32[]{:S(2)}, u32[]{:S(2)}) %all-to-all-start.1) | async-done | bytes 524320 | tf_op jit(solution)/shard_map/all_to_all | solution.py:403
  95.1 0.5 reshape.215
  95.9 1.5 reshape.216.data
  97.4 18.5 %mix.2 = (bf16[16,32,1024]{2,1,0:T(8,128)(2,1)}, bf16[16,16,1024]{2,1,0:T(8,128)(2,1)}) custom-call(bf16[64,256]{1,0:T(8,128)(2,1)} %constant.130.clone.forward, bf16[1,16,32]{2,1,0:T(8,128)(2,1)} %constant_dynamic-slice_fusion.inverse, bf16[256,1024]{1,0:T(8,128)(2,1)} %reshape.216.data, bf16[32,1024,128]{2,1,0:T(8,128)(2,1)} %bitcast.30, ...), custom_call_target="tpu_custom_call" | custom-call | tf_op jit(solution)/shard_map/mix/pallas_call | solution.py:463
  115.9 1.8 reshape.218
  117.6 0.3 copy.35
  117.9 0.6 reshape.219
  118.5 1.0 copy.28
  119.5 51.5 %layer.1 = (bf16[512,512]{1,0:T(8,128)(2,1)}, bf16[16,8,64,128]{3,2,1,0:T(8,128)(2,1)}) custom-call(bf16[512,512]{1,0:T(8,128)(2,1)} %bitcast.36, bf16[32,512,128]{2,1,0:T(8,128)(2,1)} %subtract_convert_fusion.table, f32[512,4096]{1,0:T(8,128)} %get-tuple-element.27.field, bf16[256,64]{1,0:T(8,128)(2,1)} %slice_bitcast_fusion.up, ...), custom_call_target="tpu_custom_call" | custom-call | tf_op jit(solution)/shard_map/layer/pallas_call | solution.py:492
  171.1 7.4 %all-to-all-start.2 = ((bf16[16,32,512]{2,1,0:T(8,128)(2,1)}), bf16[16,32,512]{2,1,0:T(8,128)(2,1)S(1)}, u32[]{:S(2)}, u32[]{:S(2)}) async-start(bf16[16,32,512]{2,1,0:T(8,128)(2,1)} %bitcast.39), calls=%async_computation.2 | async-start | bytes 1048576 | tf_op jit(solution)/shard_map/all_to_all | solution.py:403
  178.6 1.0 negate_convert_fusion
  179.9 0.5 copy.30
  180.5 0.3 convert_element_type.32
  180.8 0.9 copy.32.phases
  181.7 9.9 %all-to-all-done.2 = bf16[16,32,512]{2,1,0:T(8,128)(2,1)S(1)} async-done(((bf16[16,32,512]{2,1,0:T(8,128)(2,1)}), bf16[16,32,512]{2,1,0:T(8,128)(2,1)S(1)}, u32[]{:S(2)}, u32[]{:S(2)}) %all-to-all-start.2) | async-done | bytes 524320 | tf_op jit(solution)/shard_map/all_to_all | solution.py:403
  191.6 0.5 reshape.222
  192.4 1.5 reshape.223.data
  193.9 18.4 %mix.3 = (bf16[16,32,1024]{2,1,0:T(8,128)(2,1)}, bf16[16,16,1024]{2,1,0:T(8,128)(2,1)}) custom-call(bf16[64,256]{1,0:T(8,128)(2,1)} %constant.130.clone.forward, bf16[1,16,32]{2,1,0:T(8,128)(2,1)} %constant_dynamic-slice_fusion.inverse, bf16[256,1024]{1,0:T(8,128)(2,1)} %reshape.223.data, bf16[32,1024,128]{2,1,0:T(8,128)(2,1)} %bitcast.31, ...), custom_call_target="tpu_custom_call" | custom-call | tf_op jit(solution)/shard_map/mix/pallas_call | solution.py:463
  212.3 16.2 %answer.1 = f32[64,2048]{1,0:T(8,128)} custom-call(s32[64]{0:T(128)} %get-tuple-element.19.slot_of, bf16[128,64,128]{2,1,0:T(8,128)(2,1)} %bitcast.35, bf16[64,128,128]{2,1,0:T(8,128)(2,1)} %kern.3, bf16[256,512]{1,0:T(8,128)(2,1)} %copy.32.phases, bf16[1,512,1024]{2,1,0:T(8,128)(2,1)} %bitcast.37, bf16[1,512,1024]{2,1,0:T(8,128)(2,1)} %bitcast.38, ...), custom_call_target="tpu_custom_call" | custom-call | tf_op jit(solution)/shard_map/answer/pallas_call | solution.py:520
  (19 shorter events, 0.9 us)
Async XLA Ops:
  6.4 76.9 %copy-start.3 = (s32[64,1]{0,1:T(1,128)S(1)}, s32[64,1]{0,1:T(1,128)}, u32[]{:S(2)}) copy-start(s32[64,1]{0,1:T(1,128)} %param.16) | copy-start | bytes 772
  6.4 76.9 %copy-start.4 = (s32[64]{0:T(128)S(1)}, s32[64]{0:T(128)}, u32[]{:S(2)}) copy-start(s32[64]{0:T(128)} %block.1) | copy-start | bytes 772
  6.4 76.9 %copy-start.2 = (bf16[2,64,256]{2,1,0:T(8,128)(2,1)S(1)}, bf16[2,64,256]{2,1,0:T(8,128)(2,1)}, u32[]{:S(2)}) copy-start(bf16[2,64,256]{2,1,0:T(8,128)(2,1)} %down.1) | copy-start | bytes 196612
  6.4 55.0 %all-to-all-start = ((bf16[16,528,128]{2,1,0:T(8,128)(2,1)}), bf16[16,528,128]{2,1,0:T(8,128)(2,1)S(1)}, u32[]{:S(2)}, u32[]{:S(2)}) async-start(bf16[16,528,128]{2,1,0:T(8,128)(2,1)} %get-tuple-element.20), calls=%async_computation | async-start | bytes 4325376 | tf_op jit(solution)/shard_map/all_to_all | solution.py:403
  14.0 83.4 %copy-start.1 = (bf16[2,256,64]{2,1,0:T(8,128)(2,1)}, bf16[2,256,64]{2,1,0:T(8,128)(2,1)S(1)}, u32[]{:S(2)}) copy-start(bf16[2,256,64]{2,1,0:T(8,128)(2,1)S(1)} %copy.29.up) | copy-start | bytes 196612
  61.4 1.4 copy-start
  76.5 18.6 %all-to-all-start.1 = ((bf16[16,32,512]{2,1,0:T(8,128)(2,1)}), bf16[16,32,512]{2,1,0:T(8,128)(2,1)S(1)}, u32[]{:S(2)}, u32[]{:S(2)}) async-start(bf16[16,32,512]{2,1,0:T(8,128)(2,1)} %bitcast.40), calls=%async_computation.1 | async-start | bytes 1048576 | tf_op jit(solution)/shard_map/all_to_all | solution.py:403
  171.1 20.5 %all-to-all-start.2 = ((bf16[16,32,512]{2,1,0:T(8,128)(2,1)}), bf16[16,32,512]{2,1,0:T(8,128)(2,1)S(1)}, u32[]{:S(2)}, u32[]{:S(2)}) async-start(bf16[16,32,512]{2,1,0:T(8,128)(2,1)} %bitcast.39), calls=%async_computation.2 | async-start | bytes 1048576 | tf_op jit(solution)/shard_map/all_to_all | solution.py:403

commit v2 on v1

--- a/solution.py
+++ b/solution.py
@@ -221,6 +221,28 @@
         copy.wait_send()
 
 
+def mix_modes(channels, spread_of, weight, scaling, full, me):
+    rows = 2 * MX
+    width = 2 * channels
+    left = lax.broadcasted_iota(jnp.int32, (rows, width), 1) < channels
+    for pair in range(weight.shape[0] // 2):
+        halves = []
+        for k in range(2):
+            prod = jnp.dot(spread_of(2 * pair + k), weight[2 * pair + k], preferred_element_type=F32)
+            real, imag = prod[:MX], prod[MX:]
+            real_turned = pltpu.roll(real, channels, 1)
+            imag_turned = pltpu.roll(imag, channels, 1)
+            if k == 0:
+                halves.append((real - imag_turned, real_turned + imag))
+            else:
+                halves.append((real_turned - imag, real + imag_turned))
+        (real_a, imag_a), (real_b, imag_b) = halves
+        top = left[:MX]
+        both = jnp.concatenate([jnp.where(top, real_a, real_b), jnp.where(top, imag_a, imag_b)], axis=0)
+        both = (both * scaling[:, pair * width : (pair + 1) * width]).astype(BF16)
+        full[me, :, pair * width : (pair + 1) * width] = both
+
+
 def mix_kernel(number, channels, planes, depth, forward, inverse, data, weights, scaling, full, spread_out, weight, fetch_sem, *sems):
     rows = 2 * MX
     here, fan = weight.shape[0], weight.shape[1] // (2 * channels)
@@ -236,28 +258,16 @@
     modes = jnp.dot(forward[...], data[...], preferred_element_type=F32)
     modes = modes[:rows] + modes[rows:]
     fetch.wait()
-    for pair in range(here // 2):
-        own = modes[:, pair * width : (pair + 1) * width]
+
+    def spread_of(m):
+        own = modes[:, m // 2 * width : (m // 2 + 1) * width]
         other = pltpu.roll(own, channels, 1)
-        halves = []
-        for k in range(2):
-            twice = jnp.where(left, own, other) if k == 0 else jnp.where(left, other, own)
-            spread = jnp.concatenate(
-                [jnp.where(row_wave == 2 * f + half, twice, 0.0).astype(BF16) for f in range(fan)], axis=1
-            )
-            prod = jnp.dot(spread, weight[2 * pair + k], preferred_element_type=F32)
-            real, imag = prod[:MX], prod[MX:]
-            real_turned = pltpu.roll(real, channels, 1)
-            imag_turned = pltpu.roll(imag, channels, 1)
-            if k == 0:
-                halves.append((real - imag_turned, real_turned + imag))
-            else:
-                halves.append((real_turned - imag, real + imag_turned))
-        (real_a, imag_a), (real_b, imag_b) = halves
-        top = left[:MX]
-        both = jnp.concatenate([jnp.where(top, real_a, real_b), jnp.where(top, imag_a, imag_b)], axis=0)
-        both = (both * scaling[:, pair * width : (pair + 1) * width]).astype(BF16)
-        full[me, :, pair * width : (pair + 1) * width] = both
+        twice = jnp.where(left, own, other) if m % 2 == 0 else jnp.where(left, other, own)
+        return jnp.concatenate(
+            [jnp.where(row_wave == 2 * f + half, twice, 0.0).astype(BF16) for f in range(fan)], axis=1
+        )
+
+    mix_modes(channels, spread_of, weight, scaling, full, me)
 
     def arrived(block):
         spread_out[block] = jnp.dot(inverse[0], full[block], preferred_element_type=F32).astype(BF16)
@@ -271,29 +281,137 @@
     return v + v * turn
 
 
-def layer_kernel(devices, planes, wide, modes, table, field, up, down, picked, spec, fetched, total, summed, out, own_sem, send_sem, recv_sem):
+def local_table(planes, channels):
+    waves = np.arange(MX) - MX // 2
+    angle = 2 * np.pi * np.mod(np.outer(np.arange(planes), waves), NX) / NX
+    cos, sin = jnp.asarray(np.cos(angle), F32), jnp.asarray(np.sin(angle), F32)
+    parts = lax.optimization_barrier((cos, sin))
+    quarter = MX // 4
+    both = jnp.stack([a.reshape(planes, 4, quarter) for a in parts], axis=2)
+    same = (jnp.arange(channels)[:, None] == jnp.arange(channels)[None, :])[None, :, None, None, None, :]
+    wide = jnp.where(same, both[:, None, :, :, :, None], 0.0)
+    return wide.reshape(planes * channels, 4, 2 * quarter * channels).transpose(1, 0, 2).astype(BF16)
+
+
+def turn_table(devices, channels):
+    waves = np.arange(MX) - MX // 2
+    angle = 2 * np.pi * np.mod(np.outer(np.arange(devices) * (NX // devices), waves), NX) / NX
+    parts = np.stack([np.cos(angle), np.sin(angle)], axis=1)
+    return jnp.repeat(jnp.asarray(parts, F32), channels, axis=2)
+
+
+def along_modes(across, local, turns, here):
+    devices, lines = across.shape[0], across.shape[2]
+    values = across[...].reshape(devices * 2 * here, lines)
+    reals, imags = [], []
+    for q in range(local.shape[0]):
+        prod = jnp.dot(values, local[q], preferred_element_type=F32)
+        width = prod.shape[1] // 2
+        real, imag = None, None
+        for d in range(devices):
+            base = d * 2 * here
+            rc, rs = prod[base : base + here, :width], prod[base : base + here, width:]
+            ic, is_ = prod[base + here : base + 2 * here, :width], prod[base + here : base + 2 * here, width:]
+            own_real, own_imag = rc + is_, ic - rs
+            cos = turns[d, 0:1, q * width : (q + 1) * width]
+            sin = turns[d, 1:2, q * width : (q + 1) * width]
+            add_real = own_real * cos + own_imag * sin
+            add_imag = own_imag * cos - own_real * sin
+            real = add_real if real is None else real + add_real
+            imag = add_imag if imag is None else imag + add_imag
+        reals.append(real)
+        imags.append(imag)
+    return jnp.concatenate(reals, axis=1), jnp.concatenate(imags, axis=1)
+
+
+def offsets(devices):
+    return [(dz, dy, dc) for dz in range(devices // 4) for dy in range(2) for dc in range(2) if dz + dy + dc]
+
+
+def shifted(me, devices, offset, sign):
+    z, y, c = pen_position(me)
+    dz, dy, dc = offset
+    depth = devices // 4
+    return (z + (dz if sign > 0 else depth - dz)) % depth * 4 + (y + dy) % 2 * 2 + (c + dc) % 2
+
+
+def layer_kernel(
+    number, devices, planes, wide,
+    modes, table, field, up, down, local, turns, scaling, picked, weights,
+    fetched, full_out,
+    total, summed, out, spec, across, weight, full,
+    own_sem, fetch_sem, send_sem, recv_sem, spec_send, spec_recv, *sems,
+):
     channels = field.shape[0] // planes
+    here = weight.shape[0]
     me = lax.axis_index("pen")
     step, steps = pl.program_id(0), pl.num_programs(0)
+    order = offsets(devices)
+    depth = devices // 4
 
     def exchange(j):
+        peer = shifted(me, devices, order[j], 1)
         return pltpu.make_async_remote_copy(
-            src_ref=picked.at[(me + j) % devices],
+            src_ref=picked.at[peer],
             dst_ref=fetched.at[me],
             send_sem=send_sem.at[j],
             recv_sem=recv_sem.at[j],
-            device_id={"pen": (me + j) % devices},
+            device_id={"pen": peer},
             device_id_type=MESH,
         )
 
+    def arrival(j):
+        peer = shifted(me, devices, order[j], -1)
+        return pltpu.make_async_remote_copy(
+            src_ref=picked.at[peer],
+            dst_ref=fetched.at[peer],
+            send_sem=send_sem.at[j],
+            recv_sem=recv_sem.at[j],
+            device_id={"pen": peer},
+            device_id_type=MESH,
+        )
+
+    def spec_exchange(j):
+        peer = shifted(me, devices, order[j], 1)
+        return pltpu.make_async_remote_copy(
+            src_ref=spec.at[peer],
+            dst_ref=across.at[me],
+            send_sem=spec_send.at[j],
+            recv_sem=spec_recv.at[j],
+            device_id={"pen": peer},
+            device_id_type=MESH,
+        )
+
+    def spec_arrival(j):
+        peer = shifted(me, devices, order[j], -1)
+        return pltpu.make_async_remote_copy(
+            src_ref=spec.at[peer],
+            dst_ref=across.at[peer],
+            send_sem=spec_send.at[j],
+            recv_sem=spec_recv.at[j],
+            device_id={"pen": peer},
+            device_id_type=MESH,
+        )
+
+    def when_early(o):
+        dz, dy, dc = o
+        if 2 * dz < depth:
+            return 0
+        return 1 if 2 * dz > depth and dc == 0 else 2
+
+    early = [j for j, o in enumerate(order) if when_early(o) == 0 or when_early(o) == 1]
+    middle = [j for j, o in enumerate(order) if j not in early and 2 * o[0] > depth]
+    late = [j for j, o in enumerate(order) if j not in early and j not in middle]
     own = pltpu.make_async_copy(picked.at[me], fetched.at[me], own_sem)
+    fetch = pltpu.make_async_copy(weights.at[pl.ds(number * here, here)], weight, fetch_sem)
 
     @pl.when(step == 0)
     def _():
         total[...] = jnp.zeros_like(total)
-        greet([(me + j) % devices for j in range(1, devices)])
+        greet([shifted(me, devices, o, 1) for o in order])
         own.start()
-        for j in range(1, devices):
+        fetch.start()
+        for j in early:
             exchange(j).start()
 
     tile = table_tile(table, 0, wide)
@@ -316,19 +434,43 @@
 
     @pl.when(step == steps - 1)
     def _():
-        spec[...] = total[...].astype(BF16)
+        for d in range(devices):
+            spec[d] = total[d * 2 * here : (d + 1) * 2 * here, :].astype(BF16)
+        across[me] = spec[me]
+        for j in range(len(order)):
+            spec_exchange(j).start()
+        for j in middle:
+            exchange(j).start()
         own.wait()
-        for j in range(1, devices):
+        fetch.wait()
+        for j in range(len(order)):
+            spec_arrival(j).wait_recv()
+        real, imag = along_modes(across, local, turns, here)
+        lanes = MX * channels
+        keep = lax.broadcasted_iota(jnp.int32, (MX, lanes), 0) == lax.broadcasted_iota(jnp.int32, (MX, lanes), 1) // channels
+
+        def spread_of(m):
+            top = jnp.where(keep, real[m : m + 1, :], 0.0).astype(BF16)
+            low = jnp.where(keep, imag[m : m + 1, :], 0.0).astype(BF16)
+            return jnp.concatenate([top, low], axis=0)
+
+        mix_modes(channels, spread_of, weight, scaling, full, me)
+
+        def arrived(block):
+            if block is me:
+                for j in late:
+                    exchange(j).start()
+
+        gather_blocks(me, depth, full, *sems, arrived)
+        back = pltpu.make_async_copy(full, full_out, own_sem)
+        back.start()
+        for j in range(len(order)):
+            spec_exchange(j).wait_send()
+        for j in range(len(order)):
             exchange(j).wait_send()
-        for j in range(1, devices):
-            pltpu.make_async_remote_copy(
-                src_ref=picked.at[me],
-                dst_ref=fetched.at[(me + devices - j) % devices],
-                send_sem=send_sem.at[j],
-                recv_sem=recv_sem.at[j],
-                device_id={"pen": (me + devices - j) % devices},
-                device_id_type=MESH,
-            ).wait_recv()
+        for j in range(len(order)):
+            arrival(j).wait_recv()
+        back.wait()
 
 
 def point_phases(owner, block, planes, per_plane, lines_here):
@@ -455,68 +597,81 @@
     own_inverse = lax.dynamic_slice_in_dim(inverse, me, 1, axis=0)
     lines_here = size // NZ
     phases = point_phases(pair_owner[:, 0], pair_block, planes, per_plane, lines_here)
-    fulls = []
-    for number in range(LAYERS):
-        last = number == LAYERS - 1
-        across = swap(spec.reshape(devices, 2 * here, lines))
-        data = across.reshape(devices, 2, here, planes, channels).transpose(0, 1, 3, 2, 4)
-        full, modes = pl.pallas_call(
-            functools.partial(mix_kernel, number, channels, planes, depth),
-            out_shape=(
-                jax.ShapeDtypeStruct((devices, 2 * MX, here * channels), BF16),
-                jax.ShapeDtypeStruct((devices, 2 * planes, here * channels), BF16),
-            ),
-            in_specs=[VMEM, VMEM, VMEM, ANY, VMEM],
-            out_specs=(VMEM, VMEM),
-            scratch_shapes=[
-                pltpu.VMEM((here, MX * channels, 2 * channels), BF16),
-                pltpu.SemaphoreType.DMA,
-                pltpu.SemaphoreType.DMA((depth - 1,)),
-                pltpu.SemaphoreType.DMA((depth - 1,)),
-                pltpu.SemaphoreType.DMA((depth,)),
-                pltpu.SemaphoreType.DMA((depth,)),
-                pltpu.SemaphoreType.DMA((2 * depth,)),
-                pltpu.SemaphoreType.DMA((2 * depth,)),
-            ],
-            compiler_params=pltpu.CompilerParams(collective_id=number, has_side_effects=True),
-            name="mix",
-        )(forward, own_inverse, data.reshape(2 * NX, here * channels), weights, scaling)
-        fulls.append(full.reshape(MY, MZ // here, 2 * MX, here * channels).transpose(1, 0, 2, 3).reshape(MZ // here, MY * 2 * MX, here * channels))
-        if last:
-            break
-        modes = modes.reshape(devices, 2, planes, here, channels).transpose(0, 1, 3, 2, 4)
-        modes = modes.reshape(2 * modes_all, lines).T
-
-        chunk = wide * size
-        spec_shape = (2 * modes_all, lines)
-        spec, fetched = pl.pallas_call(
-            functools.partial(layer_kernel, devices, planes, wide),
-            out_shape=(
-                jax.ShapeDtypeStruct(spec_shape, BF16),
-                jax.ShapeDtypeStruct((devices, cap, channels, size), BF16),
-            ),
-            grid=(plane_cells // chunk,),
-            in_specs=[
-                pl.BlockSpec((lines, 2 * modes_all), lambda k: (0, 0)),
-                pl.BlockSpec((wide, 2 * modes_all, size), lambda k: (k, 0, 0)),
-                pl.BlockSpec((lines, chunk), lambda k: (0, k)),
-                pl.BlockSpec((hidden, channels), lambda k: (0, 0)),
-                pl.BlockSpec((channels, hidden), lambda k: (0, 0)),
-                ANY,
-            ],
-            out_specs=(pl.BlockSpec(spec_shape, lambda k: (0, 0)), ANY),
-            scratch_shapes=[
-                pltpu.VMEM(spec_shape, F32),
-                pltpu.VMEM((lines, chunk), F32),
-                pltpu.VMEM((lines, chunk), BF16),
-                pltpu.SemaphoreType.DMA,
-                pltpu.SemaphoreType.DMA((devices,)),
-                pltpu.SemaphoreType.DMA((devices,)),
-            ],
-            compiler_params=pltpu.CompilerParams(collective_id=LAYERS + number, has_side_effects=True),
-            name="layer",
-        )(modes, table, field, mlp_up[number], mlp_down[number], picked)
-
+    gather_sems = [
+        pltpu.SemaphoreType.DMA((depth - 1,)),
+        pltpu.SemaphoreType.DMA((depth - 1,)),
+        pltpu.SemaphoreType.DMA((depth,)),
+        pltpu.SemaphoreType.DMA((depth,)),
+        pltpu.SemaphoreType.DMA((2 * depth,)),
+        pltpu.SemaphoreType.DMA((2 * depth,)),
+    ]
+    full_shape = (devices, 2 * MX, here * channels)
+    weight_shape = (here, MX * channels, 2 * channels)
+    across = swap(spec.reshape(devices, 2 * here, lines))
+    data = across.reshape(devices, 2, here, planes, channels).transpose(0, 1, 3, 2, 4)
+    first, modes = pl.pallas_call(
+        functools.partial(mix_kernel, 0, channels, planes, depth),
+        out_shape=(
+            jax.ShapeDtypeStruct(full_shape, BF16),
+            jax.ShapeDtypeStruct((devices, 2 * planes, here * channels), BF16),
+        ),
+        in_specs=[VMEM, VMEM, VMEM, ANY, VMEM],
+        out_specs=(VMEM, VMEM),
+        scratch_shapes=[pltpu.VMEM(weight_shape, BF16), pltpu.SemaphoreType.DMA] + gather_sems,
+        compiler_params=pltpu.CompilerParams(collective_id=0, has_side_effects=True),
+        name="mix",
+    )(forward, own_inverse, data.reshape(2 * NX, here * channels), weights, scaling)
+    modes = modes.reshape(devices, 2, planes, here, channels).transpose(0, 1, 3, 2, 4)
+    modes = modes.reshape(2 * modes_all, lines).T
+
+    chunk = wide * size
+    local = local_table(planes, channels)
+    turns = turn_table(devices, channels)
+    whole = lambda shape: pl.BlockSpec(shape, lambda k: (0,) * len(shape))
+    peers = devices - 1
+    fetched, second = pl.pallas_call(
+        functools.partial(layer_kernel, 1, devices, planes, wide),
+        out_shape=(
+            jax.ShapeDtypeStruct((devices, cap, channels, size), BF16),
+            jax.ShapeDtypeStruct(full_shape, BF16),
+        ),
+        grid=(plane_cells // chunk,),
+        in_specs=[
+            whole((lines, 2 * modes_all)),
+            pl.BlockSpec((wide, 2 * modes_all, size), lambda k: (k, 0, 0)),
+            pl.BlockSpec((lines, chunk), lambda k: (0, k)),
+            whole((hidden, channels)),
+            whole((channels, hidden)),
+            whole(local.shape),
+            whole(turns.shape),
+            whole(scaling.shape),
+            ANY,
+            ANY,
+        ],
+        out_specs=(ANY, ANY),
+        scratch_shapes=[
+            pltpu.VMEM((2 * modes_all, lines), F32),
+            pltpu.VMEM((lines, chunk), F32),
+            pltpu.VMEM((lines, chunk), BF16),
+            pltpu.VMEM((devices, 2 * here, lines), BF16),
+            pltpu.VMEM((devices, 2 * here, lines), BF16),
+            pltpu.VMEM(weight_shape, BF16),
+            pltpu.VMEM(full_shape, BF16),
+            pltpu.SemaphoreType.DMA,
+            pltpu.SemaphoreType.DMA,
+            pltpu.SemaphoreType.DMA((peers,)),
+            pltpu.SemaphoreType.DMA((peers,)),
+            pltpu.SemaphoreType.DMA((peers,)),
+            pltpu.SemaphoreType.DMA((peers,)),
+        ]
+        + gather_sems,
+        compiler_params=pltpu.CompilerParams(collective_id=1, has_side_effects=True),
+        name="layer",
+    )(modes, table, field, mlp_up[0], mlp_down[0], local, turns, scaling, picked, weights)
+
+    groups_z = MZ // here
+    by_wave = lambda full: full.reshape(MY, groups_z, 2 * MX, here * channels).transpose(1, 0, 2, 3).reshape(groups_z, MY * 2 * MX, here * channels)
+    fulls = [by_wave(first), by_wave(second)]
     return pl.pallas_call(
         functools.partial(answer_kernel, channels, 2),
         out_shape=jax.ShapeDtypeStruct((channels, pairs // NBR * size), F32),

time: 231 us -> 216 us (0.935)
  the two profiles are of different devices: /device:TPU:17 before, /device:TPU:11 now
where the time goes in v2:
time: 216 us; the launch traced here: 215 us
  Pallas kernels  133 us (62%)
  waiting for transfers between devices  32.2 us (15%)
  local copies, waits for them, and re-layouts  24.4 us (11%)
  starting transfers between devices  13.9 us (6%)
  other arithmetic  12 us (6%)
    pallas_call x1, Pallas kernels, per_device(): pl.pallas_call(functools.partial(layer_kernel, 1, devices, planes, wide),...  79.8 us
    all_to_all x2, waiting for transfers between devices, swap(): lax.all_to_all(values, 'pen', split_axis=0, concat_axis=0, tiled=True)  32.2 us
    pallas_call x1, Pallas kernels, per_device(): pl.pallas_call(functools.partial(mix_kernel, 0, channels, planes, depth),...  16.6 us
    pallas_call x1, Pallas kernels, per_device(): pl.pallas_call(functools.partial(answer_kernel, channels, 2), out_shape=j...  16.2 us
    all_to_all x2, starting transfers between devices, swap(): lax.all_to_all(values, 'pen', split_axis=0, concat_axis=0, tiled=True)  13.9 us
    pallas_call x1, Pallas kernels, per_device(): pl.pallas_call(functools.partial(gather_sums_kernel, cap, channels, per_p...  13.6 us
    broadcast_in_dim x4, local copies, waits for them, and re-layouts, local_table(): wide = jnp.where(same, both[:, None, :, :, :, None], 0.0)  11.7 us
    convert_element_type x1, other arithmetic, plane_table(): (cos0[None] * cos_k[:, :, None] - sin0[None] * sin_k[:, :, None]).astype(...  6.48 us
  transfers between devices with their start and end apart: 2, of which 2 were waited for; matrix products, arithmetic and copies ran while one was open for 14% of the time, Pallas kernels for 0%

profile of v2, /device:TPU:11, one launch (start us, length us, event | category | flops | bytes accessed | tf_op | source)
XLA Modules:
  0.0 215.4 jit_solution(7775026191711608337)
XLA Ops:
  0.0 6.4 %encode.1 = (bf16[16,528,128]{2,1,0:T(8,128)(2,1)}, s32[64]{0:T(128)}, s32[128]{0:T(128)}) custom-call(s32[64]{0:T(128)} %bitcast.45, s32[64]{0:T(128)} %block.1, bf16[64,2048]{1,0:T(8,128)(2,1)} %feat.1, bf16[64,128,128]{2,1,0:T(8,128)(2,1)} %kern.3), custom_call_target="tpu_custom_call" | custom-call | tf_op jit(solution)/shard_map/encode/pallas_call | solution.py:564
  6.5 6.6 %all-to-all-start = ((bf16[16,528,128]{2,1,0:T(8,128)(2,1)}), bf16[16,528,128]{2,1,0:T(8,128)(2,1)S(1)}, u32[]{:S(2)}, u32[]{:S(2)}) async-start(bf16[16,528,128]{2,1,0:T(8,128)(2,1)} %get-tuple-element.21), calls=%async_computation | async-start | bytes 4325376 | tf_op jit(solution)/shard_map/all_to_all | solution.py:545
  13.5 0.8 reshape.230.turns
  14.5 1.0 negate_convert_fusion
  15.8 0.5 copy.35
  16.3 0.3 convert_element_type.39
  16.7 0.9 copy.36.phases
  17.5 0.3 broadcast_in_dim.56
  17.8 0.7 broadcast_in_dim.57
  18.5 3.1 %broadcast_in_dim.59 = bf16[8,64,4,2,4,64]{5,4,3,1,0,2:T(4,128)(2,1)} broadcast(bf16[8,4,2,4]{3,2,0,1:T(2,128)(2,1)S(1)} %copy.34), dimensions={0,2,3,4} | broadcast | bytes 2097664 | tf_op jit(solution)/shard_map/jit(_where)/broadcast_in_dim | solution.py:292
  21.6 7.7 %broadcast_in_dim.60 = bf16[512,4,512]{2,0,1:T(8,128)(2,1)} reshape(bf16[8,64,4,2,4,64]{5,4,3,1,0,2:T(4,128)(2,1)} %broadcast_in_dim.59) | data formatting | bytes 4194304 | tf_op jit(solution)/shard_map/jit(_where)/broadcast_in_dim | solution.py:292
  29.3 6.5 %subtract_convert_fusion.table = bf16[32,512,128]{2,1,0:T(8,128)(2,1)} fusion(f32[32,512]{1,0:T(8,128)S(1)} %copy-done.5, f32[512,128]{1,0:T(8,128)S(1)} %copy-done.2, f32[32,512]{1,0:T(8,128)S(1)} %copy-done.6, f32[512,128]{1,0:T(8,128)S(1)} %copy-done.3), kind=kLoop, calls=%fused_computation | loop fusion | flops 8388608 | bytes 4849664 | tf_op jit(solution)/shard_map/convert_element_type | solution.py:46
  35.8 24.7 %all-to-all-done.got = bf16[16,528,128]{2,1,0:T(8,128)(2,1)S(1)} async-done(((bf16[16,528,128]{2,1,0:T(8,128)(2,1)}), bf16[16,528,128]{2,1,0:T(8,128)(2,1)S(1)}, u32[]{:S(2)}, u32[]{:S(2)}) %all-to-all-start) | async-done | bytes 2162720 | tf_op jit(solution)/shard_map/all_to_all | solution.py:545
  60.5 0.7 reshape.232.targets
  61.2 0.6 copy-done
  61.8 13.6 %place.1 = (f32[512,4096]{1,0:T(8,128)}, bf16[512,512]{1,0:T(8,128)(2,1)}, bf16[16,8,64,128]{3,2,1,0:T(8,128)(2,1)}) custom-call(s32[128]{0:T(128)} %reshape.232.targets, bf16[16,528,128]{2,1,0:T(8,128)(2,1)} %copy-done, bf16[32,512,128]{2,1,0:T(8,128)(2,1)} %subtract_convert_fusion.table), custom_call_target="tpu_custom_call" | custom-call | tf_op jit(solution)/shard_map/place/pallas_call | solution.py:579
  75.4 7.3 %all-to-all-start.1 = ((bf16[16,32,512]{2,1,0:T(8,128)(2,1)}), bf16[16,32,512]{2,1,0:T(8,128)(2,1)S(1)}, u32[]{:S(2)}, u32[]{:S(2)}) async-start(bf16[16,32,512]{2,1,0:T(8,128)(2,1)} %bitcast.42), calls=%async_computation.1 | async-start | bytes 1048576 | tf_op jit(solution)/shard_map/all_to_all | solution.py:545
  82.7 0.6 fusion.11.scaling
  83.3 1.3 constant_dynamic-slice_fusion.inverse
  84.6 0.6 slice_bitcast_fusion.1.down
  85.2 0.6 slice_bitcast_fusion.up
  85.8 3.4 %fusion.local = bf16[4,512,512]{2,1,0:T(8,128)(2,1)} fusion(bf16[512,4,512]{2,0,1:T(8,128)(2,1)} %broadcast_in_dim.60, pred[512,512]{1,0:T(8,128)(4,1)S(1)} %broadcast_in_dim.57), kind=kLoop, calls=%fused_computation.2 | loop fusion | flops 1048576 | bytes 4456448 | tf_op jit(solution)/shard_map/convert_element_type | solution.py:293
  89.2 7.6 %all-to-all-done.1 = bf16[16,32,512]{2,1,0:T(8,128)(2,1)S(1)} async-done(((bf16[16,32,512]{2,1,0:T(8,128)(2,1)}), bf16[16,32,512]{2,1,0:T(8,128)(2,1)S(1)}, u32[]{:S(2)}, u32[]{:S(2)}) %all-to-all-start.1) | async-done | bytes 524320 | tf_op jit(solution)/shard_map/all_to_all | solution.py:545
  96.8 0.5 reshape.225
  97.6 1.5 reshape.226.data
  99.1 16.6 %mix.1 = (bf16[16,32,1024]{2,1,0:T(8,128)(2,1)}, bf16[16,16,1024]{2,1,0:T(8,128)(2,1)}) custom-call(bf16[64,256]{1,0:T(8,128)(2,1)} %constant.138.clone.forward, bf16[1,16,32]{2,1,0:T(8,128)(2,1)} %constant_dynamic-slice_fusion.inverse, bf16[256,1024]{1,0:T(8,128)(2,1)} %reshape.226.data, bf16[32,1024,128]{2,1,0:T(8,128)(2,1)} %bitcast.34, ...), custom_call_target="tpu_custom_call" | custom-call | tf_op jit(solution)/shard_map/mix/pallas_call | solution.py:612
  115.6 1.8 reshape.228
  117.4 0.3 copy.39
  117.7 0.6 reshape.229
  118.3 1.0 copy.32
  119.3 79.8 %layer.1 = (bf16[16,8,64,128]{3,2,1,0:T(8,128)(2,1)}, bf16[16,32,1024]{2,1,0:T(8,128)(2,1)}) custom-call(bf16[512,512]{1,0:T(8,128)(2,1)} %bitcast.38, bf16[32,512,128]{2,1,0:T(8,128)(2,1)} %subtract_convert_fusion.table, f32[512,4096]{1,0:T(8,128)} %get-tuple-element.28.field, bf16[256,64]{1,0:T(8,128)(2,1)} %slice_bitcast_fusion.up, ...), custom_call_target="tpu_custom_call" | custom-call | tf_op jit(solution)/shard_map/layer/pallas_call | solution.py:632
  199.2 16.2 %answer.1 = f32[64,2048]{1,0:T(8,128)} custom-call(s32[64]{0:T(128)} %get-tuple-element.20.slot_of, bf16[128,64,128]{2,1,0:T(8,128)(2,1)} %bitcast.39, bf16[64,128,128]{2,1,0:T(8,128)(2,1)} %kern.3, bf16[256,512]{1,0:T(8,128)(2,1)} %copy.36.phases, bf16[1,512,1024]{2,1,0:T(8,128)(2,1)} %bitcast.40, bf16[1,512,1024]{2,1,0:T(8,128)(2,1)} %bitcast.41, ...), custom_call_target="tpu_custom_call" | custom-call | tf_op jit(solution)/shard_map/answer/pallas_call | solution.py:675
  (39 shorter events, 1.1 us)
Async XLA Ops:
  0.0 13.0 %copy-start.9 = (bf16[8,16]{0,1:T(8,128)(2,1)S(1)}, bf16[8,16]{0,1:T(8,128)(2,1)}, u32[]{:S(2)}) copy-start(bf16[8,16]{0,1:T(8,128)(2,1)} %constant.193) | copy-start | bytes 772
  0.0 13.0 %copy-start.10 = (bf16[8,16]{0,1:T(8,128)(2,1)S(1)}, bf16[8,16]{0,1:T(8,128)(2,1)}, u32[]{:S(2)}) copy-start(bf16[8,16]{0,1:T(8,128)(2,1)} %constant.194) | copy-start | bytes 772
  0.0 13.3 %copy-start.8 = (f32[16,2,16]{2,1,0:T(2,128)S(1)}, f32[16,2,16]{2,1,0:T(2,128)}, u32[]{:S(2)}) copy-start(f32[16,2,16]{2,1,0:T(2,128)} %constant.141.clone) | copy-start | bytes 6148
  0.0 14.3 %copy-start.12 = (s32[64]{0:T(128)S(1)}, s32[64]{0:T(128)}, u32[]{:S(2)}) copy-start(s32[64]{0:T(128)} %block.1) | copy-start | bytes 772
  0.0 14.3 %copy-start.11 = (s32[64,1]{0,1:T(1,128)S(1)}, s32[64,1]{0,1:T(1,128)}, u32[]{:S(2)}) copy-start(s32[64,1]{0,1:T(1,128)} %param.19) | copy-start | bytes 772
  0.0 13.2 %copy-start.7 = (bf16[2,256,64]{1,2,0:T(8,128)(2,1)S(1)}, bf16[2,256,64]{1,2,0:T(8,128)(2,1)}, u32[]{:S(2)}) copy-start(bf16[2,256,64]{1,2,0:T(8,128)(2,1)} %param.22) | copy-start | bytes 196612
  6.5 54.0 %all-to-all-start = ((bf16[16,528,128]{2,1,0:T(8,128)(2,1)}), bf16[16,528,128]{2,1,0:T(8,128)(2,1)S(1)}, u32[]{:S(2)}, u32[]{:S(2)}) async-start(bf16[16,528,128]{2,1,0:T(8,128)(2,1)} %get-tuple-element.21), calls=%async_computation | async-start | bytes 4325376 | tf_op jit(solution)/shard_map/all_to_all | solution.py:545
  13.4 71.8 %copy-start.1 = (bf16[2,256,64]{2,1,0:T(8,128)(2,1)}, bf16[2,256,64]{2,1,0:T(8,128)(2,1)S(1)}, u32[]{:S(2)}) copy-start(bf16[2,256,64]{2,1,0:T(8,128)(2,1)S(1)} %copy.33.up) | copy-start | bytes 196612
  21.6 7.7 %copy-start.2 = (f32[512,128]{1,0:T(8,128)S(1)}, f32[512,128]{1,0:T(8,128)}, u32[]{:S(2)}) copy-start(f32[512,128]{1,0:T(8,128)} %constant.134.clone) | copy-start | bytes 786436
  21.6 7.7 %copy-start.3 = (f32[512,128]{1,0:T(8,128)S(1)}, f32[512,128]{1,0:T(8,128)}, u32[]{:S(2)}) copy-start(f32[512,128]{1,0:T(8,128)} %constant.133.clone) | copy-start | bytes 786436
  21.6 7.7 %copy-start.5 = (f32[32,512]{1,0:T(8,128)S(1)}, f32[32,512]{1,0:T(8,128)}, u32[]{:S(2)}) copy-start(f32[32,512]{1,0:T(8,128)} %constant.136.clone) | copy-start | bytes 196612
  21.6 7.7 %copy-start.6 = (f32[32,512]{1,0:T(8,128)S(1)}, f32[32,512]{1,0:T(8,128)}, u32[]{:S(2)}) copy-start(f32[32,512]{1,0:T(8,128)} %constant.135.clone) | copy-start | bytes 196612
  35.8 48.8 %copy-start.4 = (bf16[2,64,256]{2,1,0:T(8,128)(2,1)S(1)}, bf16[2,64,256]{2,1,0:T(8,128)(2,1)}, u32[]{:S(2)}) copy-start(bf16[2,64,256]{2,1,0:T(8,128)(2,1)} %down.1) | copy-start | bytes 196612
  60.4 1.3 copy-start
  75.4 21.4 %all-to-all-start.1 = ((bf16[16,32,512]{2,1,0:T(8,128)(2,1)}), bf16[16,32,512]{2,1,0:T(8,128)(2,1)S(1)}, u32[]{:S(2)}, u32[]{:S(2)}) async-start(bf16[16,32,512]{2,1,0:T(8,128)(2,1)} %bitcast.42), calls=%async_computation.1 | async-start | bytes 1048576 | tf_op jit(solution)/shard_map/all_to_all | solution.py:545

commit v3 on v2

--- a/solution.py
+++ b/solution.py
@@ -17,7 +17,6 @@
 MZ = 16
 LAYERS = 2
 NBR = 4
-NOTE_ROWS = 16
 
 F32 = jnp.float32
 BF16 = jnp.bfloat16
@@ -29,95 +28,307 @@
 ANY = pl.BlockSpec(memory_space=pl.ANY)
 
 
-def plane_table(devices, lanes):
-    here = MY * MZ // devices
-    row = np.arange(2 * MY * MZ)
-    mode = row // (2 * here) * here + row % here
-    imag = (row % (2 * here)) // here
-    wave_y = mode // MZ - MY // 2
-    wave_z = mode % MZ
-    cell = np.arange(lanes)
-    turns = np.mod(np.outer(wave_y, cell // NZ), NY) / NY + np.mod(np.outer(wave_z, cell % NZ), NZ) / NZ
-    first = 2 * np.pi * turns + np.where(imag, np.pi / 2, 0.0)[:, None]
-    tiles = NY * NZ // lanes
-    step = 2 * np.pi * np.mod(np.outer(np.arange(tiles) * (lanes // NZ), wave_y), NY) / NY
-    parts = [np.cos(first), np.sin(first), np.cos(step), np.sin(step)]
-    cos0, sin0, cos_k, sin_k = lax.optimization_barrier(tuple(jnp.asarray(a, F32) for a in parts))
-    return (cos0[None] * cos_k[:, :, None] - sin0[None] * sin_k[:, :, None]).astype(BF16)
-
-
-def along_tables(devices):
-    planes = NX // devices
-    waves = np.arange(MX) - MX // 2
-    angle = 2 * np.pi * np.mod(np.outer(waves, np.arange(NX)), NX) / NX
-    cos = np.cos(angle).reshape(MX, devices, planes)
-    sin = np.sin(angle).reshape(MX, devices, planes)
-    to_real = np.stack([cos, sin], axis=2)
-    to_imag = np.stack([-sin, cos], axis=2)
-    forward = np.concatenate([to_real, to_imag], axis=0).reshape(2 * MX, 2 * NX)
-    high = forward.astype(jnp.bfloat16).astype(np.float64)
-    both = np.concatenate([high, forward - high], axis=0)
-    own = jnp.asarray(forward.reshape(2 * MX, devices, 2 * planes).transpose(1, 2, 0), BF16)
-    return jnp.asarray(both, BF16), own
-
-
-def encode_kernel(devices, cap, owner, block, feat, kern, send, slot_of, targets, count):
-    pairs = kern.shape[0]
-    size = kern.shape[1]
+def lists_kernel(devices, cap, planes, per_plane, lines_here, owner, block, owners, blocks, order, source, slot_of, notes, xy, targets, count):
+    pairs = owner.shape[0]
 
     def clear(d, carry):
         count[d] = 0
         for i in range(cap):
             targets[d * cap + i] = -1
-        send[d] = jnp.zeros(send.shape[1:], BF16)
+            order[d * cap + i] = 0
+            source[d * cap + i] = 0
         return carry
 
     lax.fori_loop(0, devices, clear, 0)
 
-    def one(b, carry):
-        values = feat[:, pl.ds(pl.multiple_of(b * size, size), size)]
+    def one(p, carry):
+        d = owner[p]
+        n = count[d]
+        count[d] = n + 1
+        slot_of[p] = d * cap + n
+        order[d * cap + n] = p
+        source[d * cap + n] = lax.div(p, NBR)
+        targets[d * cap + n] = block[p]
+        return carry
+
+    lax.fori_loop(0, pairs, one, 0)
+    lane = lax.broadcasted_iota(jnp.int32, notes.shape[1:], 1)
+
+    def note(d, carry):
+        row = jnp.zeros(notes.shape[1:], jnp.int32)
+        for i in range(cap):
+            row = jnp.where(lane == i, targets[d * cap + i], row)
+        notes[d] = row
+        return carry
+
+    lax.fori_loop(0, devices, note, 0)
+    x = owners[...] * planes + lax.div(blocks[...], per_plane)
+    y = lax.rem(blocks[...], per_plane) * lines_here
+    xy[0:1, :] = jnp.concatenate([x] * lines_here, axis=1)
+    xy[1:2, :] = jnp.concatenate([y + i for i in range(lines_here)], axis=1)
+
+
+def turn(count, wave, place, span):
+    return lax.rem((wave + span - count // 2) * place, span).astype(F32) * (2 * math.pi / span)
+
+
+def point_phases(xy, phases):
+    lanes = xy.shape[1]
+    wave = lax.broadcasted_iota(jnp.int32, (MX, lanes), 0)
+    angle_x = turn(MX, wave, xy[0:1, :], NX)
+    cos_x, sin_x = jnp.cos(angle_x), jnp.sin(angle_x)
+    for ky in range(MY):
+        angle_y = turn(MY, jnp.full((1, lanes), ky, jnp.int32), xy[1:2, :], NY)
+        cos_y, sin_y = jnp.cos(angle_y), jnp.sin(angle_y)
+        cos = cos_x * cos_y - sin_x * sin_y
+        sin = sin_x * cos_y + cos_x * sin_y
+        top = jnp.concatenate([cos, sin], axis=1)
+        low = jnp.concatenate([-sin, cos], axis=1)
+        phases[ky * 2 * MX : (ky + 1) * 2 * MX, :] = jnp.concatenate([top, low], axis=0).astype(BF16)
+
+
+def fill_table(here, table, cos_now, sin_now, cos_step, sin_step):
+    shape = cos_now.shape
+    row = lax.broadcasted_iota(jnp.int32, shape, 0)
+    cell = lax.broadcasted_iota(jnp.int32, shape, 1)
+    mode = lax.div(row, 2 * here) * here + lax.rem(row, here)
+    imag = lax.div(lax.rem(row, 2 * here), here).astype(F32) * (math.pi / 2)
+    wave_y, wave_z = lax.div(mode, MZ), lax.rem(mode, MZ)
+    angle = turn(MY, wave_y, lax.div(cell, NZ), NY) + turn(0, wave_z, lax.rem(cell, NZ), NZ) + imag
+    cos_now[...], sin_now[...] = jnp.cos(angle), jnp.sin(angle)
+    step = turn(MY, wave_y, jnp.full(shape, shape[1] // NZ, jnp.int32), NY)
+    cos_step[...], sin_step[...] = jnp.cos(step), jnp.sin(step)
+
+    def one(k, carry):
+        cos, sin = cos_now[...], sin_now[...]
+        table[k] = cos.astype(BF16)
+        cos_now[...] = cos * cos_step[...] - sin * sin_step[...]
+        sin_now[...] = sin * cos_step[...] + cos * sin_step[...]
+        return carry
+
+    lax.fori_loop(0, table.shape[0], one, 0)
+
+
+def lay_lines(channels, planes, here, spread, lines_now, out):
+    width = 2 * channels
+    lines = planes * channels
+    left = lax.broadcasted_iota(jnp.int32, (planes, width), 1) < channels
+    keep = lax.broadcasted_iota(jnp.int32, (planes, lines), 0) == lax.broadcasted_iota(jnp.int32, (planes, lines), 1) // channels
+    picks = lax.broadcasted_iota(jnp.int32, (here, here * planes), 0) == lax.broadcasted_iota(jnp.int32, (here, here * planes), 1) // planes
+    picks = jnp.where(picks, 1.0, 0.0).astype(BF16)
+
+    def one(d, carry):
+        for half in range(2):
+            values = spread[d, half * planes : (half + 1) * planes, :]
+            pieces = []
+            for m in range(here):
+                own = values[:, m // 2 * width : (m // 2 + 1) * width]
+                other = pltpu.roll(own, channels, 1)
+                twice = jnp.where(left, own, other) if m % 2 == 0 else jnp.where(left, other, own)
+                pieces.append(jnp.where(keep, jnp.concatenate([twice] * (planes // 2), axis=1), 0.0))
+            stack = jnp.concatenate(pieces, axis=0).astype(BF16)
+            start = pl.multiple_of(d * 2 * here + half * here, here)
+            lines_now[pl.ds(start, here), :] = jnp.dot(picks, stack, preferred_element_type=F32)
+        return carry
+
+    lax.fori_loop(0, spread.shape[0], one, 0)
+    out[...] = lines_now[...].T.astype(BF16)
+
+
+def encode_kernel(
+    devices, cap, planes,
+    order, source, notes, xy, feat, kern, depths, inverse, weights,
+    got, notes_in, full_out, lines_out, phases, table_out,
+    feats, send, waves, part, part_send, from_twin, kept, side_send, from_side, line_send, from_line,
+    weight, full, spread, lines_now, table, cos_now, sin_now, cos_step, sin_step,
+    own_sem, fetch_sem, full_sem, table_sem, send_sem, recv_sem, note_send, note_recv,
+    twin_send_sem, twin_recv_sem, side_send_sem, side_recv_sem, line_send_sem, line_recv_sem, *sems,
+):
+    pairs, size = kern.shape[0], kern.shape[1]
+    channels = feat.shape[0]
+    here = weight.shape[0]
+    depth = devices // 4
+    me = lax.axis_index("pen")
+    z, y, c = pen_position(me)
+    line, side, twin = quad_partners(me, depth)
+    away = offsets(devices)
+
+    def copy_to(peer, src, dst, send_one, recv_one):
+        return pltpu.make_async_remote_copy(
+            src_ref=src, dst_ref=dst, send_sem=send_one, recv_sem=recv_one, device_id={"pen": peer}, device_id_type=MESH
+        )
+
+    def fill(peer):
+        for i in range(cap):
+            block = jnp.dot(feats[source[peer * cap + i]], kern[order[peer * cap + i]], preferred_element_type=F32)
+            send[peer, i * channels : (i + 1) * channels, :] = block.astype(BF16)
+
+    def exchange(j):
+        peer = shifted(me, devices, away[j], 1)
+        return copy_to(peer, send.at[peer], got.at[me], send_sem.at[j], recv_sem.at[j])
+
+    def arrival(j):
+        peer = shifted(me, devices, away[j], -1)
+        return copy_to(peer, send.at[peer], got.at[peer], send_sem.at[j], recv_sem.at[j])
+
+    def note_exchange(j):
+        peer = shifted(me, devices, away[j], 1)
+        return copy_to(peer, notes.at[peer], notes_in.at[me], note_send.at[j], note_recv.at[j])
+
+    def note_arrival(j):
+        peer = shifted(me, devices, away[j], -1)
+        return copy_to(peer, notes.at[peer], notes_in.at[peer], note_send.at[j], note_recv.at[j])
+
+    far = [j for j, o in enumerate(away) if 2 * o[0] == depth]
+    soon = [j for j in far if away[j][2] == 0]
+    later = [j for j in far if away[j][2] == 1]
+    rest = [j for j in range(len(away)) if j not in far]
+
+    greet([shifted(me, devices, o, 1) for o in away])
+    fetch = pltpu.make_async_copy(weights.at[pl.ds(0, here)], weight, fetch_sem)
+    fetch.start()
+    for b in range(pairs // NBR):
+        feats[b] = feat[:, b * size : (b + 1) * size]
+    for j in soon:
+        fill(shifted(me, devices, away[j], 1))
+    for j in soon:
+        exchange(j).start()
+
+    point_phases(xy, phases)
+    count = waves.shape[0] // pairs
+
+    def transform(b, carry):
+        values = feats[b]
         for k in range(NBR):
             p = b * NBR + k
-            d = owner[p]
-            n = count[d]
-            count[d] = n + 1
-            slot_of[p] = d * cap + n
-            targets[d * cap + n] = block[p]
-            rows = pl.ds(pl.multiple_of(n * values.shape[0], values.shape[0]), values.shape[0])
-            send[d, rows, :] = jnp.dot(values, kern[p], preferred_element_type=F32).astype(BF16)
-        return carry
-
-    lax.fori_loop(0, pairs // NBR, one, 0)
-    lane = lax.broadcasted_iota(jnp.int32, (NOTE_ROWS, size), 1)
-
-    def note(d, carry):
-        row = jnp.zeros((NOTE_ROWS, size), F32)
-        for i in range(cap):
-            row = jnp.where(lane == i, targets[d * cap + i].astype(F32), row)
-        send[d, send.shape[1] - NOTE_ROWS :, :] = row.astype(BF16)
-        return carry
-
-    lax.fori_loop(0, devices, note, 0)
+            block = jnp.dot(values, kern[p], preferred_element_type=F32).astype(BF16)
+            both = lax.dot_general(depths[...], block, NT, preferred_element_type=F32)
+            waves[pl.ds(p, count, stride=pairs), :] = jnp.concatenate([both[:count], both[count:]], axis=1)
+        return carry
+
+    lax.fori_loop(0, pairs // NBR, transform, 0)
+    tall = phases.shape[1]
+    lane = 2 * channels
+    groups_z, per_group = MZ // here, here // 2
+    for w in range(MZ // 2):
+        values = waves[w * tall : (w + 1) * tall, :].astype(BF16)
+        sums = jnp.dot(phases[...], values, preferred_element_type=F32)
+        cols = slice(w % per_group * lane, (w % per_group + 1) * lane)
+        for ky in range(MY):
+            d = ky * groups_z + w // per_group
+            block = sums[ky * 2 * MX : (ky + 1) * 2 * MX, :]
+            part[d, :, cols] = block
+            part_send[d, :, cols] = block.astype(BF16)
+
+    def at(z2, y2, c2):
+        return z2 * 4 + y2 * 2 + c2
+
+    walk = list(range(1, depth)) + [0]
+    sent = []
+    twins, sides, lines = {}, {}, {}
+    for s in walk:
+        z2 = (z + s) % depth
+        for f in range(2):
+            y2 = (y + 1 + f) % 2
+            twins[s, f] = copy_to(
+                twin, part_send.at[at(z2, y2, 1 - c)], from_twin.at[z2 * 2 + y2], twin_send_sem.at[2 * s + f], twin_recv_sem.at[2 * s + f]
+            )
+            twins[s, f].start()
+    for j in later:
+        fill(shifted(me, devices, away[j], 1))
+    for s in walk:
+        z2 = (z + s) % depth
+        twins[s, 0].wait_recv()
+        side_send[z2] = (part[at(z2, 1 - y, c)] + from_twin[z2 * 2 + 1 - y].astype(F32)).astype(BF16)
+        twins[s, 1].wait_recv()
+        kept[z2] = part[at(z2, y, c)] + from_twin[z2 * 2 + y].astype(F32)
+        sides[s] = copy_to(side, side_send.at[z2], from_side.at[z2], side_send_sem.at[s], side_recv_sem.at[s])
+        sides[s].start()
+    for s in walk:
+        z2 = (z + s) % depth
+        sides[s].wait_recv()
+        if s:
+            line_send[z2] = (kept[z2] + from_side[z2].astype(F32)).astype(BF16)
+            lines[s] = copy_to(at(z2, y, c), line_send.at[z2], from_line.at[z], line_send_sem.at[s - 1], line_recv_sem.at[s - 1])
+            lines[s].start()
+    for j in later:
+        exchange(j).start()
+    for j in rest:
+        fill(shifted(me, devices, away[j], 1))
+    fill(me)
+    own = pltpu.make_async_copy(send.at[me], got.at[me], own_sem)
+    own.start()
+    notes_in[me] = notes[me]
+    modes = kept[z] + from_side[z].astype(F32)
+    for s in range(1, depth):
+        z2 = (z + depth - s) % depth
+        copy_to(at(z2, y, c), line_send.at[z2], from_line.at[z2], line_send_sem.at[s - 1], line_recv_sem.at[s - 1]).wait_recv()
+        modes = modes + from_line[z2].astype(F32)
+    fetch.wait()
+
+    rows = 2 * MX
+    row_wave = lax.broadcasted_iota(jnp.int32, (rows, lane), 0) % MX
+    half = lax.broadcasted_iota(jnp.int32, (rows, lane), 1) // channels
+    left = half == 0
+    fan = MX // 2
+
+    def spread_of(m):
+        mine = modes[:, m // 2 * lane : (m // 2 + 1) * lane]
+        other = pltpu.roll(mine, channels, 1)
+        twice = jnp.where(left, mine, other) if m % 2 == 0 else jnp.where(left, other, mine)
+        return jnp.concatenate(
+            [jnp.where(row_wave == 2 * f + half, twice, 0.0).astype(BF16) for f in range(fan)], axis=1
+        )
+
+    mix_modes(channels, spread_of, weight, mode_scale(me, here, channels), full, me)
+
+    def arrived(block):
+        if block is me:
+            for j in rest:
+                exchange(j).start()
+            for j in range(len(away)):
+                note_exchange(j).start()
+        spread[block] = jnp.dot(inverse[me], full[block], preferred_element_type=F32)
+
+    gather_blocks(me, depth, full, *sems, arrived)
+    back = pltpu.make_async_copy(full, full_out, full_sem)
+    back.start()
+    lay_lines(channels, planes, here, spread, lines_now, lines_out)
+    fill_table(here, table, cos_now, sin_now, cos_step, sin_step)
+    put = pltpu.make_async_copy(table, table_out, table_sem)
+    put.start()
+    for s in walk:
+        for f in range(2):
+            twins[s, f].wait_send()
+        sides[s].wait_send()
+        if s:
+            lines[s].wait_send()
+    for j in range(len(away)):
+        note_exchange(j).wait_send()
+        note_arrival(j).wait_recv()
+        exchange(j).wait_send()
+        arrival(j).wait_recv()
+    own.wait()
+    back.wait()
+    put.wait()
 
 
 def table_tile(table, k, wide):
     return jnp.concatenate([table[k * wide + i] for i in range(wide)], axis=1)
 
 
-def gather_sums_kernel(cap, channels, per_plane, wide, targets, got, table, field, spec, send, total):
+def place_kernel(cap, channels, per_plane, targets, got, field, send):
     size = got.shape[2]
-    chunk = wide * size
-    tiles = table.shape[0] // wide
 
     def clear(k, carry):
-        field[:, pl.ds(pl.multiple_of(k * chunk, chunk), chunk)] = jnp.zeros((field.shape[0], chunk), F32)
-        return carry
-
-    lax.fori_loop(0, tiles, clear, 0)
+        field[:, pl.ds(pl.multiple_of(k * size, size), size)] = jnp.zeros((field.shape[0], size), F32)
+        return carry
+
+    lax.fori_loop(0, field.shape[1] // size, clear, 0)
 
     def add(d, carry):
         for i in range(cap):
-            t = targets[d * cap + i]
+            t = targets[d, 0, i]
 
             @pl.when(t >= 0)
             def _():
@@ -131,22 +342,13 @@
 
     def pick(d, carry):
         for i in range(cap):
-            t = jnp.maximum(targets[d * cap + i], 0)
+            t = jnp.maximum(targets[d, 0, i], 0)
             rows = pl.ds(pl.multiple_of(t // per_plane * channels, channels), channels)
             cols = pl.ds(pl.multiple_of(t % per_plane * size, size), size)
             send[d, i] = field[rows, cols].astype(BF16)
         return carry
 
     lax.fori_loop(0, got.shape[0], pick, 0)
-    total[...] = jnp.zeros_like(total)
-
-    def transform(k, carry):
-        values = field[:, pl.ds(pl.multiple_of(k * chunk, chunk), chunk)].astype(BF16)
-        total[...] += lax.dot_general(table_tile(table, k, wide), values, NT, preferred_element_type=F32)
-        return carry
-
-    lax.fori_loop(0, tiles, transform, 0)
-    spec[...] = total[...].astype(BF16)
 
 
 def pen_position(me):
@@ -243,36 +445,10 @@
         full[me, :, pair * width : (pair + 1) * width] = both
 
 
-def mix_kernel(number, channels, planes, depth, forward, inverse, data, weights, scaling, full, spread_out, weight, fetch_sem, *sems):
-    rows = 2 * MX
-    here, fan = weight.shape[0], weight.shape[1] // (2 * channels)
-    me = lax.axis_index("pen")
-    line, side, twin = quad_partners(me, depth)
-    fetch = pltpu.make_async_copy(weights.at[pl.ds(number * here, here)], weight, fetch_sem)
-    fetch.start()
-    greet(line + [side, twin])
-    width = 2 * channels
-    row_wave = lax.broadcasted_iota(jnp.int32, (rows, width), 0) % MX
-    half = lax.broadcasted_iota(jnp.int32, (rows, width), 1) // channels
-    left = half == 0
-    modes = jnp.dot(forward[...], data[...], preferred_element_type=F32)
-    modes = modes[:rows] + modes[rows:]
-    fetch.wait()
-
-    def spread_of(m):
-        own = modes[:, m // 2 * width : (m // 2 + 1) * width]
-        other = pltpu.roll(own, channels, 1)
-        twice = jnp.where(left, own, other) if m % 2 == 0 else jnp.where(left, other, own)
-        return jnp.concatenate(
-            [jnp.where(row_wave == 2 * f + half, twice, 0.0).astype(BF16) for f in range(fan)], axis=1
-        )
-
-    mix_modes(channels, spread_of, weight, scaling, full, me)
-
-    def arrived(block):
-        spread_out[block] = jnp.dot(inverse[0], full[block], preferred_element_type=F32).astype(BF16)
-
-    gather_blocks(me, depth, full, *sems, arrived)
+def mode_scale(me, here, channels):
+    cell = lax.broadcasted_iota(jnp.int32, (1, here * channels), 1)
+    wave_z = lax.rem(me * here + lax.div(cell, channels), MZ)
+    return jnp.where(wave_z == 0, 1.0, 2.0) * (1.0 / (NX * NY * NZ))
 
 
 def gelu_twice(v):
@@ -281,16 +457,20 @@
     return v + v * turn
 
 
-def local_table(planes, channels):
+def local_rows(planes, channels):
     waves = np.arange(MX) - MX // 2
     angle = 2 * np.pi * np.mod(np.outer(np.arange(planes), waves), NX) / NX
-    cos, sin = jnp.asarray(np.cos(angle), F32), jnp.asarray(np.sin(angle), F32)
-    parts = lax.optimization_barrier((cos, sin))
     quarter = MX // 4
-    both = jnp.stack([a.reshape(planes, 4, quarter) for a in parts], axis=2)
-    same = (jnp.arange(channels)[:, None] == jnp.arange(channels)[None, :])[None, :, None, None, None, :]
-    wide = jnp.where(same, both[:, None, :, :, :, None], 0.0)
-    return wide.reshape(planes * channels, 4, 2 * quarter * channels).transpose(1, 0, 2).astype(BF16)
+    both = np.stack([np.cos(angle).reshape(planes, 4, quarter), np.sin(angle).reshape(planes, 4, quarter)], axis=2)
+    return jnp.asarray(np.repeat(both.reshape(planes, 4, 2 * quarter), channels, axis=2).transpose(1, 0, 2), F32)
+
+
+def fill_local(channels, rows, local):
+    lanes = rows.shape[2]
+    same = lax.broadcasted_iota(jnp.int32, (channels, lanes), 0) == lax.broadcasted_iota(jnp.int32, (channels, lanes), 1) % channels
+    for q in range(rows.shape[0]):
+        for p in range(rows.shape[1]):
+            local[q, p * channels : (p + 1) * channels, :] = jnp.where(same, rows[q, p : p + 1, :], 0.0).astype(BF16)
 
 
 def turn_table(devices, channels):
@@ -337,9 +517,9 @@
 
 def layer_kernel(
     number, devices, planes, wide,
-    modes, table, field, up, down, local, turns, scaling, picked, weights,
+    modes, table, field, up, down, local_small, turns, picked, weights,
     fetched, full_out,
-    total, summed, out, spec, across, weight, full,
+    total, summed, out, spec, across, weight, full, local,
     own_sem, fetch_sem, send_sem, recv_sem, spec_send, spec_recv, *sems,
 ):
     channels = field.shape[0] // planes
@@ -413,6 +593,7 @@
         fetch.start()
         for j in early:
             exchange(j).start()
+        fill_local(channels, local_small, local)
 
     tile = table_tile(table, 0, wide)
     summed[...] = field[...] + jnp.dot(modes[...], tile, preferred_element_type=F32)
@@ -454,7 +635,7 @@
             low = jnp.where(keep, imag[m : m + 1, :], 0.0).astype(BF16)
             return jnp.concatenate([top, low], axis=0)
 
-        mix_modes(channels, spread_of, weight, scaling, full, me)
+        mix_modes(channels, spread_of, weight, mode_scale(me, here, channels), full, me)
 
         def arrived(block):
             if block is me:
@@ -473,21 +654,6 @@
         back.wait()
 
 
-def point_phases(owner, block, planes, per_plane, lines_here):
-    x = owner * planes + block // per_plane
-    y = (block % per_plane)[None, :] * lines_here + jnp.arange(lines_here, dtype=jnp.int32)[:, None]
-    wave_x = jnp.arange(MX, dtype=jnp.int32) - MX // 2
-    wave_y = jnp.arange(MY, dtype=jnp.int32) - MY // 2
-    turns_x = jnp.mod(x[:, None] * wave_x[None, :], NX).astype(F32) / NX
-    turns_y = jnp.mod(y[:, :, None] * wave_y[None, None, :], NY).astype(F32) / NY
-    angle = 2 * math.pi * (turns_x[None, :, None, :] + turns_y[:, :, :, None])
-    cos, sin = jnp.cos(angle), jnp.sin(angle)
-    real = jnp.stack([cos, -sin], axis=3)
-    imag = jnp.stack([sin, cos], axis=3)
-    rows = 2 * lines_here * x.shape[0]
-    return jnp.stack([real, imag], axis=0).reshape(rows, MY * 2 * MX).astype(BF16)
-
-
 def depth_table(size):
     lines_here = size // NZ
     wave = np.arange(MZ)
@@ -503,13 +669,14 @@
 def answer_kernel(channels, group, slot_of, got, kern, phases, first, second, depths, up, down, out, waves):
     size = kern.shape[1]
     pairs = kern.shape[0]
-    tall = phases.shape[0]
+    turned = phases[...].T
+    tall = turned.shape[0]
     lane = 2 * channels
     per_group = first.shape[2] // lane
     for number, full in enumerate((first, second)):
         for g in range(full.shape[0]):
             for w in range(per_group):
-                part = jnp.dot(phases[...], full[g, :, w * lane : (w + 1) * lane], preferred_element_type=F32)
+                part = jnp.dot(turned, full[g, :, w * lane : (w + 1) * lane], preferred_element_type=F32)
                 start = (g * per_group + w) * tall
                 waves[number, start : start + tall, :] = part
     count = waves.shape[1] // pairs
@@ -541,8 +708,14 @@
     lax.fori_loop(0, pairs // NBR // group, body, 0)
 
 
-def swap(values):
-    return lax.all_to_all(values, "pen", split_axis=0, concat_axis=0, tiled=True)
+def plane_inverse(devices):
+    planes = NX // devices
+    waves = np.arange(MX) - MX // 2
+    angle = 2 * np.pi * np.mod(np.outer(np.arange(NX), waves), NX) / NX
+    cos, sin = np.cos(angle).reshape(devices, planes, MX), np.sin(angle).reshape(devices, planes, MX)
+    real = np.concatenate([cos, -sin], axis=2)
+    imag = np.concatenate([sin, cos], axis=2)
+    return jnp.asarray(np.concatenate([real, imag], axis=1), BF16)
 
 
 def per_device(point_feat, pair_kernel, pair_owner, pair_block, spec_weight, mlp_up, mlp_down):
@@ -558,83 +731,107 @@
     hidden = mlp_up.shape[1]
     lines = planes * channels
     wide = 4
-    table = plane_table(devices, size)
-    forward, inverse = along_tables(devices)
-
-    send, slot_of, targets = pl.pallas_call(
-        functools.partial(encode_kernel, devices, cap),
+    lines_here = size // NZ
+    depth = devices // 4
+    peers = devices - 1
+    waves_tall = 2 * lines_here * pairs
+    DMA = pltpu.SemaphoreType.DMA
+    shape = jax.ShapeDtypeStruct
+    weights = spec_weight.reshape(LAYERS * here, MX * channels, 2 * channels)
+    depths = depth_table(size)
+    depth_rows = depths.shape[0]
+    forward_depths = depths.reshape(depth_rows, 2, size).transpose(1, 0, 2).reshape(2 * depth_rows, size)
+    owner = pair_owner[:, 0]
+
+    order, source, slot_of, notes, xy = pl.pallas_call(
+        functools.partial(lists_kernel, devices, cap, planes, per_plane, lines_here),
         out_shape=(
-            jax.ShapeDtypeStruct((devices, cap * channels + NOTE_ROWS, size), BF16),
-            jax.ShapeDtypeStruct((pairs,), jnp.int32),
-            jax.ShapeDtypeStruct((devices * cap,), jnp.int32),
+            shape((devices * cap,), jnp.int32),
+            shape((devices * cap,), jnp.int32),
+            shape((pairs,), jnp.int32),
+            shape((devices, 8, 128), jnp.int32),
+            shape((2, lines_here * pairs), jnp.int32),
         ),
         in_specs=[SMEM, SMEM, VMEM, VMEM],
-        out_specs=(VMEM, SMEM, SMEM),
-        scratch_shapes=[pltpu.SMEM((devices,), jnp.int32)],
-        name="encode",
-    )(pair_owner[:, 0], pair_block, point_feat, pair_kernel)
-    got = swap(send)
-    wanted = got[:, cap * channels, :cap].astype(jnp.int32).reshape(devices * cap)
-
-    field, spec, picked = pl.pallas_call(
-        functools.partial(gather_sums_kernel, cap, channels, per_plane, wide),
-        out_shape=(
-            jax.ShapeDtypeStruct((lines, plane_cells), F32),
-            jax.ShapeDtypeStruct((2 * modes_all, lines), BF16),
-            jax.ShapeDtypeStruct((devices, cap, channels, size), BF16),
-        ),
-        in_specs=[SMEM, VMEM, VMEM],
-        out_specs=(VMEM, VMEM, VMEM),
-        scratch_shapes=[pltpu.VMEM((2 * modes_all, lines), F32)],
-        name="place",
-    )(wanted, got, table)
-
-    me = lax.axis_index("pen")
-    depth = devices // 4
-    wave_z = (me * here + jnp.arange(here * channels, dtype=jnp.int32) // channels) % MZ
-    scaling = (jnp.where(wave_z == 0, 1.0, 2.0).astype(F32) / (NX * NY * NZ))[None, :]
-    weights = spec_weight.reshape(LAYERS * here, MX * channels, 2 * channels)
-    own_inverse = lax.dynamic_slice_in_dim(inverse, me, 1, axis=0)
-    lines_here = size // NZ
-    phases = point_phases(pair_owner[:, 0], pair_block, planes, per_plane, lines_here)
-    gather_sems = [
-        pltpu.SemaphoreType.DMA((depth - 1,)),
-        pltpu.SemaphoreType.DMA((depth - 1,)),
-        pltpu.SemaphoreType.DMA((depth,)),
-        pltpu.SemaphoreType.DMA((depth,)),
-        pltpu.SemaphoreType.DMA((2 * depth,)),
-        pltpu.SemaphoreType.DMA((2 * depth,)),
-    ]
+        out_specs=(SMEM, SMEM, SMEM, VMEM, VMEM),
+        scratch_shapes=[pltpu.SMEM((devices * cap,), jnp.int32), pltpu.SMEM((devices,), jnp.int32)],
+        name="lists",
+    )(owner, pair_block, owner.reshape(1, pairs), pair_block.reshape(1, pairs))
+
+    gather_sems = [DMA((depth - 1,)), DMA((depth - 1,)), DMA((depth,)), DMA((depth,)), DMA((2 * depth,)), DMA((2 * depth,))]
     full_shape = (devices, 2 * MX, here * channels)
     weight_shape = (here, MX * channels, 2 * channels)
-    across = swap(spec.reshape(devices, 2 * here, lines))
-    data = across.reshape(devices, 2, here, planes, channels).transpose(0, 1, 3, 2, 4)
-    first, modes = pl.pallas_call(
-        functools.partial(mix_kernel, 0, channels, planes, depth),
+    table_shape = (plane_cells // size, 2 * modes_all, size)
+    block_shape = full_shape[1:]
+    trig = pltpu.VMEM((2 * modes_all, size), F32)
+    got, wanted, first, modes, phases, table = pl.pallas_call(
+        functools.partial(encode_kernel, devices, cap, planes),
         out_shape=(
-            jax.ShapeDtypeStruct(full_shape, BF16),
-            jax.ShapeDtypeStruct((devices, 2 * planes, here * channels), BF16),
+            shape((devices, cap * channels, size), BF16),
+            shape((devices, 8, 128), jnp.int32),
+            shape(full_shape, BF16),
+            shape((lines, 2 * modes_all), BF16),
+            shape((MY * 2 * MX, waves_tall), BF16),
+            shape(table_shape, BF16),
         ),
-        in_specs=[VMEM, VMEM, VMEM, ANY, VMEM],
+        in_specs=[SMEM] * 2 + [VMEM] * 6 + [ANY],
+        out_specs=(ANY, VMEM, ANY, VMEM, VMEM, ANY),
+        scratch_shapes=[
+            pltpu.VMEM((pairs // NBR, channels, size), BF16),
+            pltpu.VMEM((devices, cap * channels, size), BF16),
+            pltpu.VMEM((MZ // 2 * waves_tall, 2 * channels), F32),
+            pltpu.VMEM(full_shape, F32),
+            pltpu.VMEM(full_shape, BF16),
+            pltpu.VMEM((2 * depth,) + block_shape, BF16),
+            pltpu.VMEM((depth,) + block_shape, F32),
+            pltpu.VMEM((depth,) + block_shape, BF16),
+            pltpu.VMEM((depth,) + block_shape, BF16),
+            pltpu.VMEM((depth,) + block_shape, BF16),
+            pltpu.VMEM((depth,) + block_shape, BF16),
+            pltpu.VMEM(weight_shape, BF16),
+            pltpu.VMEM(full_shape, BF16),
+            pltpu.VMEM((devices, 2 * planes, here * channels), F32),
+            pltpu.VMEM((2 * modes_all, lines), F32),
+            pltpu.VMEM(table_shape, BF16),
+            trig,
+            trig,
+            trig,
+            trig,
+            DMA,
+            DMA,
+            DMA,
+            DMA,
+            DMA((peers,)),
+            DMA((peers,)),
+            DMA((peers,)),
+            DMA((peers,)),
+            DMA((2 * depth,)),
+            DMA((2 * depth,)),
+            DMA((depth,)),
+            DMA((depth,)),
+            DMA((depth - 1,)),
+            DMA((depth - 1,)),
+        ]
+        + gather_sems,
+        compiler_params=pltpu.CompilerParams(collective_id=0, has_side_effects=True),
+        name="encode",
+    )(order, source, notes, xy, point_feat, pair_kernel, forward_depths, plane_inverse(devices), weights)
+
+    field, picked = pl.pallas_call(
+        functools.partial(place_kernel, cap, channels, per_plane),
+        out_shape=(shape((lines, plane_cells), F32), shape((devices, cap, channels, size), BF16)),
+        in_specs=[SMEM, VMEM],
         out_specs=(VMEM, VMEM),
-        scratch_shapes=[pltpu.VMEM(weight_shape, BF16), pltpu.SemaphoreType.DMA] + gather_sems,
-        compiler_params=pltpu.CompilerParams(collective_id=0, has_side_effects=True),
-        name="mix",
-    )(forward, own_inverse, data.reshape(2 * NX, here * channels), weights, scaling)
-    modes = modes.reshape(devices, 2, planes, here, channels).transpose(0, 1, 3, 2, 4)
-    modes = modes.reshape(2 * modes_all, lines).T
+        name="place",
+    )(wanted, got)
 
     chunk = wide * size
-    local = local_table(planes, channels)
+    local_small = local_rows(planes, channels)
     turns = turn_table(devices, channels)
-    whole = lambda shape: pl.BlockSpec(shape, lambda k: (0,) * len(shape))
-    peers = devices - 1
+    whole = lambda extent: pl.BlockSpec(extent, lambda k: (0,) * len(extent))
     fetched, second = pl.pallas_call(
         functools.partial(layer_kernel, 1, devices, planes, wide),
-        out_shape=(
-            jax.ShapeDtypeStruct((devices, cap, channels, size), BF16),
-            jax.ShapeDtypeStruct(full_shape, BF16),
-        ),
+        out_shape=(shape((devices, cap, channels, size), BF16), shape(full_shape, BF16)),
         grid=(plane_cells // chunk,),
         in_specs=[
             whole((lines, 2 * modes_all)),
@@ -642,9 +839,8 @@
             pl.BlockSpec((lines, chunk), lambda k: (0, k)),
             whole((hidden, channels)),
             whole((channels, hidden)),
-            whole(local.shape),
+            whole(local_small.shape),
             whole(turns.shape),
-            whole(scaling.shape),
             ANY,
             ANY,
         ],
@@ -657,29 +853,29 @@
             pltpu.VMEM((devices, 2 * here, lines), BF16),
             pltpu.VMEM(weight_shape, BF16),
             pltpu.VMEM(full_shape, BF16),
-            pltpu.SemaphoreType.DMA,
-            pltpu.SemaphoreType.DMA,
-            pltpu.SemaphoreType.DMA((peers,)),
-            pltpu.SemaphoreType.DMA((peers,)),
-            pltpu.SemaphoreType.DMA((peers,)),
-            pltpu.SemaphoreType.DMA((peers,)),
+            pltpu.VMEM((local_small.shape[0], lines, local_small.shape[2]), BF16),
+            DMA,
+            DMA,
+            DMA((peers,)),
+            DMA((peers,)),
+            DMA((peers,)),
+            DMA((peers,)),
         ]
         + gather_sems,
         compiler_params=pltpu.CompilerParams(collective_id=1, has_side_effects=True),
         name="layer",
-    )(modes, table, field, mlp_up[0], mlp_down[0], local, turns, scaling, picked, weights)
+    )(modes, table, field, mlp_up[0], mlp_down[0], local_small, turns, picked, weights)
 
     groups_z = MZ // here
     by_wave = lambda full: full.reshape(MY, groups_z, 2 * MX, here * channels).transpose(1, 0, 2, 3).reshape(groups_z, MY * 2 * MX, here * channels)
-    fulls = [by_wave(first), by_wave(second)]
     return pl.pallas_call(
         functools.partial(answer_kernel, channels, 2),
-        out_shape=jax.ShapeDtypeStruct((channels, pairs // NBR * size), F32),
+        out_shape=shape((channels, pairs // NBR * size), F32),
         in_specs=[SMEM] + [VMEM] * 8,
         out_specs=VMEM,
-        scratch_shapes=[pltpu.VMEM((LAYERS, MZ // 2 * 2 * lines_here * pairs, 2 * channels), F32)],
+        scratch_shapes=[pltpu.VMEM((LAYERS, MZ // 2 * waves_tall, 2 * channels), F32)],
         name="answer",
-    )(slot_of, fetched.reshape(devices * cap, channels, size), pair_kernel, phases, *fulls, depth_table(size), mlp_up, mlp_down)
+    )(slot_of, fetched.reshape(devices * cap, channels, size), pair_kernel, phases, by_wave(first), by_wave(second), depths, mlp_up, mlp_down)
 
 
 def solution(mesh):

time: 216 us -> 184 us (0.85)
  the two profiles are of different devices: /device:TPU:11 before, /device:TPU:9 now
where the time goes in v3:
time: 184 us
  Pallas kernels  179 us (97%)
  local copies, waits for them, and re-layouts  4.67 us (3%)
    pallas_call x1, Pallas kernels, per_device(): pl.pallas_call(functools.partial(layer_kernel, 1, devices, planes, wide),...  78 us
    pallas_call x1, Pallas kernels, per_device(): pl.pallas_call(functools.partial(encode_kernel, devices, cap, planes), ou...  72.3 us
    pallas_call x1, Pallas kernels, per_device(): pl.pallas_call(functools.partial(answer_kernel, channels, 2), out_shape=s...  16.3 us
    pallas_call x1, Pallas kernels, per_device(): pl.pallas_call(functools.partial(place_kernel, cap, channels, per_plane),...  9.46 us

profile of v3, /device:TPU:9, one launch (start us, length us, event | category | flops | bytes accessed | tf_op | source)
XLA Modules:
  0.0 183.5 jit_solution(7898983073047407760)
XLA Ops:
  0.0 1.4 slice_bitcast_fusion.1.down
  1.4 2.8 %lists.1 = (s32[128]{0:T(128)}, s32[128]{0:T(128)}, s32[64]{0:T(128)}, s32[16,8,128]{2,1,0:T(8,128)}, s32[2,128]{1,0:T(2,128)}) custom-call(s32[64]{0:T(128)} %bitcast.18, s32[64]{0:T(128)} %block.1, s32[1,64]{1,0:T(1,128)} %bitcast.19, s32[1,64]{1,0:T(1,128)} %bitcast.20), custom_call_target="tpu_custom_call" | custom-call | tf_op jit(solution)/shard_map/lists/pallas_call | solution.py:746
  4.1 1.0 copy.12.up
  5.1 0.0 copy-start
  5.1 0.7 slice_bitcast_fusion.up
  5.8 0.8 broadcast_in_dim.3
  6.6 0.8 reshape.22.turns
  7.5 72.3 %encode.1 = (bf16[16,512,128]{2,1,0:T(8,128)(2,1)}, s32[16,8,128]{2,1,0:T(8,128)}, bf16[16,32,1024]{2,1,0:T(8,128)(2,1)}, bf16[512,512]{1,0:T(8,128)(2,1)}, bf16...) custom-call(s32[128]{0:T(128)} %get-tuple-element.21.order, s32[128]{0:T(128)} %get-tuple-element.22.source, ...), custom_call_target="tpu_custom_call" | custom-call | tf_op jit(solution)/shard_map/encode/pallas_call | solution.py:767
  79.7 0.0 copy-done
  79.7 9.5 %place.1 = (f32[512,4096]{1,0:T(8,128)}, bf16[16,8,64,128]{3,2,1,0:T(8,128)(2,1)}) custom-call(s32[16,8,128]{2,1,0:T(8,128)} %get-tuple-element.27.targets, bf16[16,512,128]{2,1,0:T(8,128)(2,1)} %get-tuple-element.28.got), custom_call_target="tpu_custom_call" | custom-call | tf_op jit(solution)/shard_map/place/pallas_call | solution.py:820
  89.2 78.0 %layer.1 = (bf16[16,8,64,128]{3,2,1,0:T(8,128)(2,1)}, bf16[16,32,1024]{2,1,0:T(8,128)(2,1)}) custom-call(bf16[512,512]{1,0:T(8,128)(2,1)} %get-tuple-element.25.modes, bf16[32,512,128]{2,1,0:T(8,128)(2,1)} %get-tuple-element.26.table, f32[512,4096]{1,0:T(8,128)} %get-tuple-element.29.field, bf16[256,64]{1,0:T(8,128)(2,1)} %slice_bitcast_fusion.up, ...), custom_call_target="tpu_custom_call" | custom-call | tf_op jit(solution)/shard_map/layer/pallas_call | solution.py:832
  167.2 16.3 %answer.1 = f32[64,2048]{1,0:T(8,128)} custom-call(s32[64]{0:T(128)} %get-tuple-element.20.slot_of, bf16[128,64,128]{2,1,0:T(8,128)(2,1)} %bitcast.15, bf16[64,128,128]{2,1,0:T(8,128)(2,1)} %kern.3, bf16[512,256]{1,0:T(8,128)(2,1)} %get-tuple-element.32.phases, bf16[1,512,1024]{2,1,0:T(8,128)(2,1)} %bitcast.16, bf16[1,512,1024]{2,1,0:T(8,128)(2,1)} %bitcast.17, ...), custom_call_target="tpu_custom_call" | custom-call | tf_op jit(solution)/shard_map/answer/pallas_call | solution.py:871
Async XLA Ops:
  5.1 74.6 %copy-start = (bf16[2,256,64]{2,1,0:T(8,128)(2,1)}, bf16[2,256,64]{2,1,0:T(8,128)(2,1)S(1)}, u32[]{:S(2)}) copy-start(bf16[2,256,64]{2,1,0:T(8,128)(2,1)S(1)} %copy.12.up) | copy-start | bytes 196612

commit v4 on v3

v4 whole, which is shorter than its diff:
```python
import functools
import math

import jax
import jax.numpy as jnp
import numpy as np
from jax import lax
from jax.experimental import pallas as pl
from jax.experimental.pallas import tpu as pltpu
from jax.sharding import PartitionSpec as P

NX = 128
NY = 64
NZ = 64
MX = 16
MY = 16
MZ = 16
LAYERS = 2
NBR = 4

F32 = jnp.float32
BF16 = jnp.bfloat16
VMEM = pl.BlockSpec(memory_space=pltpu.VMEM)
SMEM = pl.BlockSpec(memory_space=pltpu.SMEM)
NT = (((1,), (1,)), ((), ()))
TN = (((0,), (0,)), ((), ()))
MESH = pl.DeviceIdType.MESH
ANY = pl.BlockSpec(memory_space=pl.ANY)


def lists_kernel(devices, cap, planes, per_plane, lines_here, owner, block, owners, blocks, order, source, slot_of, notes, xy, slots_xy, targets, count):
    pairs = owner.shape[0]

    def clear(d, carry):
        count[d] = 0
        for i in range(cap):
            targets[d * cap + i] = -1
            order[d * cap + i] = 0
            source[d * cap + i] = 0
        return carry

    lax.fori_loop(0, devices, clear, 0)

    def one(p, carry):
        d = owner[p]
        n = count[d]
        count[d] = n + 1
        slot_of[p] = d * cap + n
        order[d * cap + n] = p
        source[d * cap + n] = lax.div(p, NBR)
        targets[d * cap + n] = block[p]
        return carry

    lax.fori_loop(0, pairs, one, 0)
    lane = lax.broadcasted_iota(jnp.int32, notes.shape[1:], 1)

    def note(d, carry):
        row = jnp.zeros(notes.shape[1:], jnp.int32)
        for i in range(cap):
            row = jnp.where(lane == i, targets[d * cap + i], row)
        notes[d] = row
        return carry

    lax.fori_loop(0, devices, note, 0)
    x = owners[...] * planes + lax.div(blocks[...], per_plane)
    y = lax.rem(blocks[...], per_plane) * lines_here
    xy[0:1, :] = jnp.concatenate([x] * lines_here, axis=1)
    xy[1:2, :] = jnp.concatenate([y + i for i in range(lines_here)], axis=1)
    places = lax.broadcasted_iota(jnp.int32, (1, devices * cap), 1)
    row = jnp.zeros((1, devices * cap), jnp.int32)
    for i in range(devices * cap):
        row = jnp.where(places == i, jnp.maximum(targets[i], 0), row)
    x = lax.div(places, cap) * planes + lax.div(row, per_plane)
    y = lax.rem(row, per_plane) * lines_here
    slots_xy[0:1, :] = jnp.concatenate([x] * lines_here, axis=1)
    slots_xy[1:2, :] = jnp.concatenate([y + i for i in range(lines_here)], axis=1)


def turn(count, wave, place, span):
    return lax.rem((wave + span - count // 2) * place, span).astype(F32) * (2 * math.pi / span)


def point_phases(xy, phases):
    lanes = xy.shape[1]
    wave = lax.broadcasted_iota(jnp.int32, (MX, lanes), 0)
    angle_x = turn(MX, wave, xy[0:1, :], NX)
    cos_x, sin_x = jnp.cos(angle_x), jnp.sin(angle_x)
    for ky in range(MY):
        angle_y = turn(MY, jnp.full((1, lanes), ky, jnp.int32), xy[1:2, :], NY)
        cos_y, sin_y = jnp.cos(angle_y), jnp.sin(angle_y)
        cos = cos_x * cos_y - sin_x * sin_y
        sin = sin_x * cos_y + cos_x * sin_y
        top = jnp.concatenate([cos, sin], axis=1)
        low = jnp.concatenate([-sin, cos], axis=1)
        phases[ky * 2 * MX : (ky + 1) * 2 * MX, :] = jnp.concatenate([top, low], axis=0).astype(BF16)


def fill_table(here, table, cos_now, sin_now, cos_step, sin_step):
    shape = cos_now.shape
    row = lax.broadcasted_iota(jnp.int32, shape, 0)
    cell = lax.broadcasted_iota(jnp.int32, shape, 1)
    mode = lax.div(row, 2 * here) * here + lax.rem(row, here)
    imag = lax.div(lax.rem(row, 2 * here), here).astype(F32) * (math.pi / 2)
    wave_y, wave_z = lax.div(mode, MZ), lax.rem(mode, MZ)
    angle = turn(MY, wave_y, lax.div(cell, NZ), NY) + turn(0, wave_z, lax.rem(cell, NZ), NZ) + imag
    cos_now[...], sin_now[...] = jnp.cos(angle), jnp.sin(angle)
    step = turn(MY, wave_y, jnp.full(shape, shape[1] // NZ, jnp.int32), NY)
    cos_step[...], sin_step[...] = jnp.cos(step), jnp.sin(step)

    def one(k, carry):
        cos, sin = cos_now[...], sin_now[...]
        table[k] = cos.astype(BF16)
        cos_now[...] = cos * cos_step[...] - sin * sin_step[...]
        sin_now[...] = sin * cos_step[...] + cos * sin_step[...]
        return carry

    lax.fori_loop(0, table.shape[0], one, 0)


def lay_lines(channels, planes, here, spread, lines_now, out):
    width = 2 * channels
    lines = planes * channels
    left = lax.broadcasted_iota(jnp.int32, (planes, width), 1) < channels
    keep = lax.broadcasted_iota(jnp.int32, (planes, lines), 0) == lax.broadcasted_iota(jnp.int32, (planes, lines), 1) // channels
    picks = lax.broadcasted_iota(jnp.int32, (here, here * planes), 0) == lax.broadcasted_iota(jnp.int32, (here, here * planes), 1) // planes
    picks = jnp.where(picks, 1.0, 0.0).astype(BF16)

    def one(d, carry):
        for half in range(2):
            values = spread[d, half * planes : (half + 1) * planes, :]
            pieces = []
            for m in range(here):
                own = values[:, m // 2 * width : (m // 2 + 1) * width]
                other = pltpu.roll(own, channels, 1)
                twice = jnp.where(left, own, other) if m % 2 == 0 else jnp.where(left, other, own)
                pieces.append(jnp.where(keep, jnp.concatenate([twice] * (planes // 2), axis=1), 0.0))
            stack = jnp.concatenate(pieces, axis=0).astype(BF16)
            start = pl.multiple_of(d * 2 * here + half * here, here)
            lines_now[pl.ds(start, here), :] = jnp.dot(picks, stack, preferred_element_type=F32)
        return carry

    lax.fori_loop(0, spread.shape[0], one, 0)
    out[...] = lines_now[...].T.astype(BF16)


def encode_kernel(
    devices, cap, planes,
    order, source, notes, xy, feat, kern, depths, inverse, weights,
    got, notes_in, full_out, lines_out, table_out,
    phases, feats, send, waves, part, part_send, from_twin, kept, side_send, from_side, line_send, from_line,
    weight, full, spread, lines_now, table, cos_now, sin_now, cos_step, sin_step,
    own_sem, fetch_sem, full_sem, table_sem, send_sem, recv_sem, note_send, note_recv, *sems,
):
    pairs, size = kern.shape[0], kern.shape[1]
    channels = feat.shape[0]
    here = weight.shape[0]
    depth = devices // 4
    me = lax.axis_index("pen")
    away = offsets(devices)

    def fill(peer):
        for i in range(cap):
            block = jnp.dot(feats[source[peer * cap + i]], kern[order[peer * cap + i]], preferred_element_type=F32)
            send[peer, i * channels : (i + 1) * channels, :] = block.astype(BF16)

    def exchange(j):
        peer = shifted(me, devices, away[j], 1)
        return copy_to(peer, send.at[peer], got.at[me], send_sem.at[j], recv_sem.at[j])

    def arrival(j):
        peer = shifted(me, devices, away[j], -1)
        return copy_to(peer, send.at[peer], got.at[peer], send_sem.at[j], recv_sem.at[j])

    def note_exchange(j):
        peer = shifted(me, devices, away[j], 1)
        return copy_to(peer, notes.at[peer], notes_in.at[me], note_send.at[j], note_recv.at[j])

    def note_arrival(j):
        peer = shifted(me, devices, away[j], -1)
        return copy_to(peer, notes.at[peer], notes_in.at[peer], note_send.at[j], note_recv.at[j])

    first_set, second_set, third_set, last_set = [], [], [], []
    for j, (dz, dy, dc) in enumerate(away):
        if 2 * dz != depth:
            last_set.append(j)
        elif dc == 0:
            first_set.append(j)
        elif dy == 0:
            second_set.append(j)
        else:
            third_set.append(j)

    def fill_all(chosen):
        for j in chosen:
            fill(shifted(me, devices, away[j], 1))

    def start_all(chosen):
        for j in chosen:
            exchange(j).start()

    greet([shifted(me, devices, o, 1) for o in away])
    fetch = pltpu.make_async_copy(weights.at[pl.ds(0, here)], weight, fetch_sem)
    fetch.start()
    for b in range(pairs // NBR):
        feats[b] = feat[:, b * size : (b + 1) * size]
    fill_all(first_set)
    start_all(first_set)

    point_phases(xy, phases)
    count = waves.shape[0] // pairs

    def transform(b, carry):
        values = feats[b]
        for k in range(NBR):
            p = b * NBR + k
            block = jnp.dot(values, kern[p], preferred_element_type=F32).astype(BF16)
            both = lax.dot_general(depths[...], block, NT, preferred_element_type=F32)
            waves[pl.ds(p, count, stride=pairs), :] = jnp.concatenate([both[:count], both[count:]], axis=1)
        return carry

    lax.fori_loop(0, pairs // NBR, transform, 0)
    tall = phases.shape[1]
    lane = 2 * channels
    groups_z, per_group = MZ // here, here // 2
    for w in range(MZ // 2):
        values = waves[w * tall : (w + 1) * tall, :].astype(BF16)
        sums = jnp.dot(phases[...], values, preferred_element_type=F32)
        cols = slice(w % per_group * lane, (w % per_group + 1) * lane)
        for ky in range(MY):
            d = ky * groups_z + w // per_group
            block = sums[ky * 2 * MX : (ky + 1) * 2 * MX, :]
            part[d, :, cols] = block
            part_send[d, :, cols] = block.astype(BF16)

    own = pltpu.make_async_copy(send.at[me], got.at[me], own_sem)

    def filler():
        fill_all(second_set)
        start_all(second_set)
        fill_all(third_set)

    def pushed():
        start_all(third_set)
        fill_all(last_set)
        fill(me)
        own.start()
        notes_in[me] = notes[me]
        fetch.wait()

    modes, sent = reduce_blocks(
        me, depth, part, part_send, from_twin, kept, side_send, from_side, line_send, from_line, sems[:6], filler, pushed
    )

    rows = 2 * MX
    row_wave = lax.broadcasted_iota(jnp.int32, (rows, lane), 0) % MX
    half = lax.broadcasted_iota(jnp.int32, (rows, lane), 1) // channels
    left = half == 0
    fan = MX // 2

    def spread_of(m):
        mine = modes[:, m // 2 * lane : (m // 2 + 1) * lane]
        other = pltpu.roll(mine, channels, 1)
        twice = jnp.where(left, mine, other) if m % 2 == 0 else jnp.where(left, other, mine)
        return jnp.concatenate(
            [jnp.where(row_wave == 2 * f + half, twice, 0.0).astype(BF16) for f in range(fan)], axis=1
        )

    mix_modes(channels, spread_of, weight, mode_scale(me, here, channels), full, me)

    def arrived(i, block):
        if i == 0:
            start_all(last_set)
            for j in range(len(away)):
                note_exchange(j).start()
        spread[block] = jnp.dot(inverse[me], full[block], preferred_element_type=F32)

    sent = sent + gather_blocks(me, depth, full, *sems[6:], arrived)
    back = pltpu.make_async_copy(full, full_out, full_sem)
    back.start()
    lay_lines(channels, planes, here, spread, lines_now, lines_out)
    fill_table(here, table, cos_now, sin_now, cos_step, sin_step)
    put = pltpu.make_async_copy(table, table_out, table_sem)
    put.start()
    for copy in sent:
        copy.wait_send()
    for j in range(len(away)):
        note_exchange(j).wait_send()
        note_arrival(j).wait_recv()
        exchange(j).wait_send()
        arrival(j).wait_recv()
    own.wait()
    back.wait()
    put.wait()


def table_tile(table, k, wide):
    return jnp.concatenate([table[k * wide + i] for i in range(wide)], axis=1)


def place_kernel(cap, channels, per_plane, targets, got, field, send):
    size = got.shape[2]

    def clear(k, carry):
        field[:, pl.ds(pl.multiple_of(k * size, size), size)] = jnp.zeros((field.shape[0], size), F32)
        return carry

    lax.fori_loop(0, field.shape[1] // size, clear, 0)

    def add(d, carry):
        for i in range(cap):
            t = targets[d, 0, i]

            @pl.when(t >= 0)
            def _():
                rows = pl.ds(pl.multiple_of(t // per_plane * channels, channels), channels)
                cols = pl.ds(pl.multiple_of(t % per_plane * size, size), size)
                field[rows, cols] += got[d, i * channels : (i + 1) * channels, :].astype(F32)

        return carry

    lax.fori_loop(0, got.shape[0], add, 0)

    def pick(d, carry):
        for i in range(cap):
            t = jnp.maximum(targets[d, 0, i], 0)
            rows = pl.ds(pl.multiple_of(t // per_plane * channels, channels), channels)
            cols = pl.ds(pl.multiple_of(t % per_plane * size, size), size)
            send[d, i] = field[rows, cols].astype(BF16)
        return carry

    lax.fori_loop(0, got.shape[0], pick, 0)


def pen_position(me):
    return me // 4, me // 2 % 2, me % 2


def greet(partners):
    barrier = pltpu.get_barrier_semaphore()
    for d in partners:
        pl.semaphore_signal(barrier, inc=1, device_id={"pen": d}, device_id_type=MESH)
    pl.semaphore_wait(barrier, len(partners))


def flip(z, mask):
    bit = 1
    while bit <= mask:
        if mask & bit:
            z = z + bit * (1 - 2 * (z // bit % 2))
        bit *= 2
    return z


def at(z, y, c):
    return z * 4 + y * 2 + c


def copy_to(peer, src, dst, send_sem, recv_sem):
    return pltpu.make_async_remote_copy(
        src_ref=src, dst_ref=dst, send_sem=send_sem, recv_sem=recv_sem, device_id={"pen": peer}, device_id_type=MESH
    )


def low_bit(mask):
    return mask & -mask


def reduce_blocks(me, depth, part, part_send, from_twin, kept, side_send, from_side, line_send, from_line, sems, filler, pushed):
    twin_send_sem, twin_recv_sem, side_send_sem, side_recv_sem, line_send_sem, line_recv_sem = sems
    z, y, c = pen_position(me)
    side, twin = at(z, 1 - y, c), at(z, y, 1 - c)
    walk = sorted(range(depth), key=lambda m: (low_bit(m) or depth, m))
    sent = []

    def start(copy):
        copy.start()
        sent.append(copy)
        return copy

    twins, sides, lines = {}, {}, {}
    for m in walk:
        z2 = flip(z, m)
        for f in range(2):
            y2 = (y + 1 + f) % 2
            k = 2 * m + f
            twins[m, f] = start(
                copy_to(twin, part_send.at[at(z2, y2, 1 - c)], from_twin.at[z2 * 2 + y2], twin_send_sem.at[k], twin_recv_sem.at[k])
            )
    filler()
    for m in walk:
        z2 = flip(z, m)
        twins[m, 0].wait_recv()
        side_send[z2] = (part[at(z2, 1 - y, c)] + from_twin[z2 * 2 + 1 - y].astype(F32)).astype(BF16)
        twins[m, 1].wait_recv()
        kept[z2] = part[at(z2, y, c)] + from_twin[z2 * 2 + y].astype(F32)
        sides[m] = start(copy_to(side, side_send.at[z2], from_side.at[z2], side_send_sem.at[m], side_recv_sem.at[m]))

    def push(m):
        line_send[m - 1] = kept[flip(z, m)].astype(BF16)
        peer = at(flip(z, low_bit(m)), y, c)
        lines[m] = start(copy_to(peer, line_send.at[m - 1], from_line.at[m - 1], line_send_sem.at[m - 1], line_recv_sem.at[m - 1]))

    for m in walk:
        z2 = flip(z, m)
        sides[m].wait_recv()
        kept[z2] = kept[z2] + from_side[z2].astype(F32)
        if m % 2:
            push(m)
    stride = 1
    while stride < depth:
        for m in range(1, depth):
            if low_bit(m) == stride:
                lines[m].wait_recv()
                z2 = flip(z, m - stride)
                kept[z2] = kept[z2] + from_line[m - 1].astype(F32)
        stride *= 2
        for m in range(1, depth):
            if low_bit(m) == stride:
                push(m)
        if 2 * stride == depth:
            pushed()
    return kept[z], sent


def gather_blocks(me, depth, full, z_send, z_recv, y_send, y_recv, c_send, c_recv, arrived):
    z, y, c = pen_position(me)
    side, twin = at(z, 1 - y, c), at(z, y, 1 - c)
    strides = [depth >> (i + 1) for i in range(depth.bit_length() - 1)]
    started = []

    def push(block, target, send_sem, recv_sem):
        copy = copy_to(target, full.at[block], full.at[block], send_sem, recv_sem)
        copy.start()
        started.append(copy)

    def landed(block, send_sem, recv_sem):
        copy_to(twin, full.at[block], full.at[block], send_sem, recv_sem).wait_recv()

    def mask_of(i):
        return sum(strides[b] for b in range(len(strides)) if i >> b & 1)

    def onward(i, level):
        block = at(flip(z, mask_of(i)), y, c)
        for deeper in range(level, len(strides)):
            k = (1 << deeper) + i - 1
            push(block, at(flip(z, strides[deeper]), y, c), z_send.at[k], z_recv.at[k])
        push(block, side, y_send.at[i], y_recv.at[i])
        push(block, twin, c_send.at[i], c_recv.at[i])
        arrived(i, block)

    onward(0, 0)
    for i in range(1, depth):
        landed(at(flip(z, mask_of(i)), y, c), z_send.at[i - 1], z_recv.at[i - 1])
        onward(i, i.bit_length())
    for i in range(depth):
        block = at(flip(z, mask_of(i)), 1 - y, c)
        landed(block, y_send.at[i], y_recv.at[i])
        push(block, twin, c_send.at[depth + i], c_recv.at[depth + i])
        arrived(depth + i, block)
    for i in range(2 * depth):
        block = at(flip(z, mask_of(i % depth)), y if i < depth else 1 - y, 1 - c)
        landed(block, c_send.at[i], c_recv.at[i])
        arrived(2 * depth + i, block)
    return started


def mix_modes(channels, spread_of, weight, scaling, full, me):
    rows = 2 * MX
    width = 2 * channels
    left = lax.broadcasted_iota(jnp.int32, (rows, width), 1) < channels
    for pair in range(weight.shape[0] // 2):
        halves = []
        for k in range(2):
            prod = jnp.dot(spread_of(2 * pair + k), weight[2 * pair + k], preferred_element_type=F32)
            real, imag = prod[:MX], prod[MX:]
            real_turned = pltpu.roll(real, channels, 1)
            imag_turned = pltpu.roll(imag, channels, 1)
            if k == 0:
                halves.append((real - imag_turned, real_turned + imag))
            else:
                halves.append((real_turned - imag, real + imag_turned))
        (real_a, imag_a), (real_b, imag_b) = halves
        top = left[:MX]
        both = jnp.concatenate([jnp.where(top, real_a, real_b), jnp.where(top, imag_a, imag_b)], axis=0)
        both = (both * scaling[:, pair * width : (pair + 1) * width]).astype(BF16)
        full[me, :, pair * width : (pair + 1) * width] = both


def mode_scale(me, here, channels):
    cell = lax.broadcasted_iota(jnp.int32, (1, here * channels), 1)
    wave_z = lax.rem(me * here + lax.div(cell, channels), MZ)
    return jnp.where(wave_z == 0, 1.0, 2.0) * (1.0 / (NX * NY * NZ))


def gelu_twice(v):
    scale = math.sqrt(2.0 / math.pi)
    turn = jnp.tanh(v * (BF16(scale) + BF16(scale * 0.044715) * (v * v)))
    return v + v * turn


def local_rows(planes, channels):
    waves = np.arange(MX) - MX // 2
    angle = 2 * np.pi * np.mod(np.outer(np.arange(planes), waves), NX) / NX
    quarter = MX // 4
    both = np.stack([np.cos(angle).reshape(planes, 4, quarter), np.sin(angle).reshape(planes, 4, quarter)], axis=2)
    return jnp.asarray(np.repeat(both.reshape(planes, 4, 2 * quarter), channels, axis=2).transpose(1, 0, 2), F32)


def fill_local(channels, rows, local):
    lanes = rows.shape[2]
    same = lax.broadcasted_iota(jnp.int32, (channels, lanes), 0) == lax.broadcasted_iota(jnp.int32, (channels, lanes), 1) % channels
    for q in range(rows.shape[0]):
        for p in range(rows.shape[1]):
            local[q, p * channels : (p + 1) * channels, :] = jnp.where(same, rows[q, p : p + 1, :], 0.0).astype(BF16)


def turn_table(devices, channels):
    waves = np.arange(MX) - MX // 2
    angle = 2 * np.pi * np.mod(np.outer(np.arange(devices) * (NX // devices), waves), NX) / NX
    parts = np.stack([np.cos(angle), np.sin(angle)], axis=1)
    return jnp.asarray(np.repeat(parts, channels, axis=2), F32)


def along_parts(spec, local, turns, me, here, part, part_send):
    devices = part.shape[0]
    values = spec[...].astype(BF16)
    for q in range(local.shape[0]):
        prod = jnp.dot(values, local[q], preferred_element_type=F32)
        width = prod.shape[1] // 2
        cols = slice(q * width, (q + 1) * width)
        cos, sin = turns[me, 0:1, cols], turns[me, 1:2, cols]
        for d in range(devices):
            base = d * 2 * here
            real_rows, imag_rows = prod[base : base + here], prod[base + here : base + 2 * here]
            own_real = real_rows[:, :width] + imag_rows[:, width:]
            own_imag = imag_rows[:, :width] - real_rows[:, width:]
            block = jnp.concatenate([own_real * cos + own_imag * sin, own_imag * cos - own_real * sin], axis=0)
            part[d, :, cols] = block
            part_send[d, :, cols] = block.astype(BF16)


def offsets(devices):
    return [(dz, dy, dc) for dz in range(devices // 4) for dy in range(2) for dc in range(2) if dz + dy + dc]


def shifted(me, devices, offset, sign):
    z, y, c = pen_position(me)
    dz, dy, dc = offset
    depth = devices // 4
    return (z + (dz if sign > 0 else depth - dz)) % depth * 4 + (y + dy) % 2 * 2 + (c + dc) % 2


def wide_gelu_twice(v):
    scale = math.sqrt(2.0 / math.pi)
    turn = jnp.tanh(v * (scale + scale * 0.044715 * (v * v)))
    return (v + v * turn).astype(BF16)


def make_waves(turned, full, waves, number, channels):
    tall, lane = turned.shape[0], 2 * channels
    devices = full.shape[0]
    groups_z = devices // MY
    per_group = full.shape[2] // lane
    for w in range(MZ // 2):
        g, cols = w // per_group, slice(w % per_group * lane, (w % per_group + 1) * lane)
        rows = jnp.concatenate([full[ky * groups_z + g, :, cols] for ky in range(MY)], axis=0)
        waves[number, w * tall : (w + 1) * tall, :] = jnp.dot(turned[...], rows, preferred_element_type=F32)


def layer_kernel(
    devices, planes, wide, cap,
    slot_of, modes, table, field, ups, downs, local_small, turns, depths, slots_xy, picked, weights, first_in, kern_in,
    answer,
    total, summed, out, part, part_send, from_twin, kept, side_send, from_side, line_send, from_line,
    weight, first, second, local, fetched, kern, phases, turned, waves, results, up, down,
    own_sem, fetch_sem, first_sem, kern_sem, send_sem, recv_sem, *sems,
):
    channels = field.shape[0] // planes
    here = weight.shape[0]
    size = kern.shape[1]
    pairs = kern.shape[0]
    me = lax.axis_index("pen")
    step, steps = pl.program_id(0), pl.num_programs(0)
    order = offsets(devices)
    depth = devices // 4

    def exchange(j):
        peer = shifted(me, devices, order[j], 1)
        return copy_to(peer, picked.at[peer], fetched.at[me], send_sem.at[j], recv_sem.at[j])

    early, second_set, third_set, last_set = [], [], [], []
    for j, (dz, dy, dc) in enumerate(order):
        if 2 * dz < depth or (2 * dz > depth and dc == 0):
            early.append(j)
        elif 2 * dz > depth or (dy == 0 and dc == 0):
            second_set.append(j)
        elif dc == 0:
            third_set.append(j)
        else:
            last_set.append(j)

    def start_all(chosen):
        for j in chosen:
            exchange(j).start()

    own = pltpu.make_async_copy(picked.at[me], fetched.at[me], own_sem)
    fetch = pltpu.make_async_copy(weights.at[pl.ds(here, here)], weight, fetch_sem)
    fetch_first = pltpu.make_async_copy(first_in, first, first_sem)
    fetch_kern = pltpu.make_async_copy(kern_in, kern, kern_sem)

    @pl.when(step == 0)
    def _():
        greet([shifted(me, devices, o, 1) for o in order])
        start_all(early)
        own.start()
        fetch.start()
        fetch_first.start()
        fetch_kern.start()
        total[...] = jnp.zeros_like(total)
        for n in range(LAYERS):
            up[n] = ups[n].T
            down[n] = (downs[n].astype(F32) * 0.5).astype(BF16)
        fill_local(channels, local_small, local)
        point_phases(slots_xy, phases)

    tile = table_tile(table, 0, wide)
    summed[...] = field[...] + jnp.dot(modes[...], tile, preferred_element_type=F32)

    def raise_up(p):
        values = summed[p * channels : (p + 1) * channels, :]
        return jnp.dot(up[0], values.astype(BF16), preferred_element_type=F32).astype(BF16)

    ahead = raise_up(0)
    for p in range(planes):
        v = ahead
        if p + 1 < planes:
            ahead = raise_up(p + 1)
        rows = slice(p * channels, (p + 1) * channels)
        values = summed[rows, :] + jnp.dot(down[0], gelu_twice(v), preferred_element_type=F32)
        out[rows, :] = values.astype(BF16)
    total[...] += lax.dot_general(tile, out[...], NT, preferred_element_type=F32)

    @pl.when(step == steps - 1)
    def _():
        start_all(second_set)
        along_parts(total, local, turns, me, here, part, part_send)

        def filler():
            fetch_first.wait()
            turned[...] = phases[...].T
            make_waves(turned, first, waves, 0, channels)

        def pushed():
            start_all(third_set)
            fetch.wait()
            own.wait()
            fetch_kern.wait()

        spectrum, sent = reduce_blocks(
            me, depth, part, part_send, from_twin, kept, side_send, from_side, line_send, from_line, sems[:6], filler, pushed
        )
        lanes = MX * channels
        keep = lax.broadcasted_iota(jnp.int32, (MX, lanes), 0) == lax.broadcasted_iota(jnp.int32, (MX, lanes), 1) // channels

        def spread_of(m):
            top = jnp.where(keep, spectrum[m : m + 1, :], 0.0).astype(BF16)
            low = jnp.where(keep, spectrum[here + m : here + m + 1, :], 0.0).astype(BF16)
            return jnp.concatenate([top, low], axis=0)

        mix_modes(channels, spread_of, weight, mode_scale(me, here, channels), second, me)

        def arrived(i, block):
            if i == 0:
                start_all(last_set)

        sent = sent + gather_blocks(me, depth, second, *sems[6:], arrived)
        make_waves(turned, second, waves, 1, channels)
        slots = devices * cap
        count = waves.shape[1] // slots

        def spectral(number, slot):
            value = waves[number, pl.ds(slot, count, stride=slots), :].astype(BF16)
            both = lax.dot_general(value, depths[...], TN, preferred_element_type=F32)
            return both[:channels, :size] + both[channels:, size:]

        def finish(peer):
            values = jnp.concatenate([fetched[peer, i].astype(F32) for i in range(cap)], axis=1)
            for n in range(LAYERS):
                now = values + jnp.concatenate([spectral(n, peer * cap + i) for i in range(cap)], axis=1)
                v = jnp.dot(up[n], now.astype(BF16), preferred_element_type=F32)
                values = now + jnp.dot(down[n], wide_gelu_twice(v), preferred_element_type=F32)
            values = values.astype(BF16)
            for i in range(cap):
                results[peer * cap + i] = values[:, i * size : (i + 1) * size]

        def take(t, carry):
            peer = shifted(me, devices, (t // 4, t // 2 % 2, t % 2), -1)

            @pl.when(t > 0)
            def _():
                copy_to(peer, picked.at[peer], fetched.at[peer], send_sem.at[t - 1], recv_sem.at[t - 1]).wait_recv()

            finish(peer)
            return carry

        middle = depth // 2
        lax.fori_loop(0, 4 * middle, take, 0)
        beyond = 2 * (depth - middle - 1)
        lax.fori_loop(0, 2 * beyond, lambda i, carry: take(4 * (middle + 1) + i % beyond * 2 + i // beyond, carry), 0)
        lax.fori_loop(0, 4, lambda i, carry: take(4 * middle + i % 2 * 2 + i // 2, carry), 0)

        def project(b, carry):
            acc = None
            for k in range(NBR):
                p = b * NBR + k
                term = lax.dot_general(results[slot_of[p]], kern[p], NT, preferred_element_type=F32)
                acc = term if acc is None else acc + term
            answer[:, pl.ds(pl.multiple_of(b * size, size), size)] = acc
            return carry

        lax.fori_loop(0, pairs // NBR, project, 0)
        for copy in sent:
            copy.wait_send()
        for j in range(len(order)):
            exchange(j).wait_send()


def depth_table(size):
    lines_here = size // NZ
    wave = np.arange(MZ)
    cell = np.arange(size)
    angle = 2 * np.pi * np.mod(np.outer(wave, cell % NZ), NZ) / NZ
    on_line = (cell // NZ)[None, :] == np.arange(lines_here)[:, None]
    parts = np.stack([np.cos(angle), -np.sin(angle)], axis=1)
    full = parts[:, :, None, :] * on_line[None, None, :, :]
    full = full.reshape(MZ // 2, 2, 2 * lines_here, size).transpose(0, 2, 1, 3)
    return jnp.asarray(full.reshape(MZ // 2 * 2 * lines_here, 2 * size), BF16)


def plane_inverse(devices):
    planes = NX // devices
    waves = np.arange(MX) - MX // 2
    angle = 2 * np.pi * np.mod(np.outer(np.arange(NX), waves), NX) / NX
    cos, sin = np.cos(angle).reshape(devices, planes, MX), np.sin(angle).reshape(devices, planes, MX)
    real = np.concatenate([cos, -sin], axis=2)
    imag = np.concatenate([sin, cos], axis=2)
    return jnp.asarray(np.concatenate([real, imag], axis=1), BF16)


def per_device(point_feat, pair_kernel, pair_owner, pair_block, spec_weight, mlp_up, mlp_down):
    devices = lax.axis_size("pen")
    pairs, size = pair_kernel.shape[0], pair_kernel.shape[1]
    channels = point_feat.shape[0]
    cap = 2 * pairs // devices
    planes = NX // devices
    plane_cells = NY * NZ
    per_plane = plane_cells // size
    here = spec_weight.shape[1]
    modes_all = MY * MZ
    lines = planes * channels
    wide = 4
    lines_here = size // NZ
    depth = devices // 4
    peers = devices - 1
    waves_tall = 2 * lines_here * pairs
    DMA = pltpu.SemaphoreType.DMA
    shape = jax.ShapeDtypeStruct
    weights = spec_weight.reshape(LAYERS * here, MX * channels, 2 * channels)
    depths = depth_table(size)
    depth_rows = depths.shape[0]
    forward_depths = depths.reshape(depth_rows, 2, size).transpose(1, 0, 2).reshape(2 * depth_rows, size)
    owner = pair_owner[:, 0]

    order, source, slot_of, notes, xy, slots_xy = pl.pallas_call(
        functools.partial(lists_kernel, devices, cap, planes, per_plane, lines_here),
        out_shape=(
            shape((devices * cap,), jnp.int32),
            shape((devices * cap,), jnp.int32),
            shape((pairs,), jnp.int32),
            shape((devices, 8, 128), jnp.int32),
            shape((2, lines_here * pairs), jnp.int32),
            shape((2, lines_here * devices * cap), jnp.int32),
        ),
        in_specs=[SMEM, SMEM, VMEM, VMEM],
        out_specs=(SMEM, SMEM, SMEM, VMEM, VMEM, VMEM),
        scratch_shapes=[pltpu.SMEM((devices * cap,), jnp.int32), pltpu.SMEM((devices,), jnp.int32)],
        name="lists",
    )(owner, pair_block, owner.reshape(1, pairs), pair_block.reshape(1, pairs))

    gather_sems = [DMA((depth - 1,)), DMA((depth - 1,)), DMA((depth,)), DMA((depth,)), DMA((2 * depth,)), DMA((2 * depth,))]
    full_shape = (devices, 2 * MX, here * channels)
    weight_shape = (here, MX * channels, 2 * channels)
    table_shape = (plane_cells // size, 2 * modes_all, size)
    block_shape = full_shape[1:]
    trig = pltpu.VMEM((2 * modes_all, size), F32)
    reduce_scratch = [
        pltpu.VMEM((2 * depth,) + block_shape, BF16),
        pltpu.VMEM((depth,) + block_shape, F32),
        pltpu.VMEM((depth,) + block_shape, BF16),
        pltpu.VMEM((depth,) + block_shape, BF16),
        pltpu.VMEM((depth - 1,) + block_shape, BF16),
        pltpu.VMEM((depth - 1,) + block_shape, BF16),
    ]
    reduce_sems = [DMA((2 * depth,)), DMA((2 * depth,)), DMA((depth,)), DMA((depth,)), DMA((depth - 1,)), DMA((depth - 1,))]
    got, wanted, first, modes, table = pl.pallas_call(
        functools.partial(encode_kernel, devices, cap, planes),
        out_shape=(
            shape((devices, cap * channels, size), BF16),
            shape((devices, 8, 128), jnp.int32),
            shape(full_shape, BF16),
            shape((lines, 2 * modes_all), BF16),
            shape(table_shape, BF16),
        ),
        in_specs=[SMEM] * 2 + [VMEM] * 6 + [ANY],
        out_specs=(ANY, VMEM, ANY, VMEM, ANY),
        scratch_shapes=[
            pltpu.VMEM((MY * 2 * MX, waves_tall), BF16),
            pltpu.VMEM((pairs // NBR, channels, size), BF16),
            pltpu.VMEM((devices, cap * channels, size), BF16),
            pltpu.VMEM((MZ // 2 * waves_tall, 2 * channels), F32),
            pltpu.VMEM(full_shape, F32),
            pltpu.VMEM(full_shape, BF16),
        ]
        + reduce_scratch
        + [
            pltpu.VMEM(weight_shape, BF16),
            pltpu.VMEM(full_shape, BF16),
            pltpu.VMEM((devices, 2 * planes, here * channels), F32),
            pltpu.VMEM((2 * modes_all, lines), F32),
            pltpu.VMEM(table_shape, BF16),
            trig,
            trig,
            trig,
            trig,
            DMA,
            DMA,
            DMA,
            DMA,
            DMA((peers,)),
            DMA((peers,)),
            DMA((peers,)),
            DMA((peers,)),
        ]
        + reduce_sems
        + gather_sems,
        compiler_params=pltpu.CompilerParams(collective_id=0, has_side_effects=True),
        name="encode",
    )(order, source, notes, xy, point_feat, pair_kernel, forward_depths, plane_inverse(devices), weights)

    field, picked = pl.pallas_call(
        functools.partial(place_kernel, cap, channels, per_plane),
        out_shape=(shape((lines, plane_cells), F32), shape((devices, cap, channels, size), BF16)),
        in_specs=[SMEM, VMEM],
        out_specs=(VMEM, VMEM),
        name="place",
    )(wanted, got)

    chunk = wide * size
    local_small = local_rows(planes, channels)
    turns = turn_table(devices, channels)
    whole = lambda extent: pl.BlockSpec(extent, lambda k: (0,) * len(extent))
    slots = devices * cap
    part_shape = (devices, 2 * here, MX * channels)
    line_shape = part_shape[1:]
    return pl.pallas_call(
        functools.partial(layer_kernel, devices, planes, wide, cap),
        out_shape=shape((channels, pairs // NBR * size), F32),
        grid=(plane_cells // chunk,),
        in_specs=[
            SMEM,
            whole((lines, 2 * modes_all)),
            pl.BlockSpec((wide, 2 * modes_all, size), lambda k: (k, 0, 0)),
            pl.BlockSpec((lines, chunk), lambda k: (0, k)),
            whole((LAYERS,) + mlp_up.shape[:0:-1]),
            whole(mlp_down.shape),
            whole(local_small.shape),
            whole(turns.shape),
            whole(depths.shape),
            whole(slots_xy.shape),
            ANY,
            ANY,
            ANY,
            ANY,
        ],
        out_specs=whole((channels, pairs // NBR * size)),
        scratch_shapes=[
            pltpu.VMEM((2 * modes_all, lines), F32),
            pltpu.VMEM((lines, chunk), F32),
            pltpu.VMEM((lines, chunk), BF16),
            pltpu.VMEM(part_shape, F32),
            pltpu.VMEM(part_shape, BF16),
            pltpu.VMEM((2 * depth,) + line_shape, BF16),
            pltpu.VMEM((depth,) + line_shape, F32),
            pltpu.VMEM((depth,) + line_shape, BF16),
            pltpu.VMEM((depth,) + line_shape, BF16),
            pltpu.VMEM((depth - 1,) + line_shape, BF16),
            pltpu.VMEM((depth - 1,) + line_shape, BF16),
            pltpu.VMEM(weight_shape, BF16),
            pltpu.VMEM(full_shape, BF16),
            pltpu.VMEM(full_shape, BF16),
            pltpu.VMEM((local_small.shape[0], lines, local_small.shape[2]), BF16),
            pltpu.VMEM((devices, cap, channels, size), BF16),
            pltpu.VMEM(pair_kernel.shape, BF16),
            pltpu.VMEM((MY * 2 * MX, 2 * lines_here * slots), BF16),
            pltpu.VMEM((2 * lines_here * slots, MY * 2 * MX), BF16),
            pltpu.VMEM((LAYERS, MZ // 2 * 2 * lines_here * slots, 2 * channels), F32),
            pltpu.VMEM((slots, channels, size), BF16),
            pltpu.VMEM(mlp_up.shape, BF16),
            pltpu.VMEM(mlp_down.shape, BF16),
            DMA,
            DMA,
            DMA,
            DMA,
            DMA((peers,)),
            DMA((peers,)),
        ]
        + reduce_sems
        + gather_sems,
        compiler_params=pltpu.CompilerParams(collective_id=1, has_side_effects=True),
        name="layer",
    )(slot_of, modes, table, field, mlp_up.transpose(0, 2, 1), mlp_down, local_small, turns, depths, slots_xy, picked, weights, first, pair_kernel)


def solution(mesh):
    in_specs = (
        P(None, ("groups", "pen")),
        P(("groups", "pen"), None, None),
        P(("groups", "pen"), None),
        P(("groups", "pen")),
        P(None, "pen", None, None, None),
        P(),
        P(),
    )
    out_specs = P(None, ("groups", "pen"))
    return jax.shard_map(
        per_device, mesh=mesh, in_specs=in_specs, out_specs=out_specs, check_vma=False
    )
```

time: 184 us -> 189 us (1.027)
  the two profiles are of different devices: /device:TPU:9 before, /device:TPU:17 now
where the time goes in v4:
time: 189 us; the launch traced here: 188 us
  Pallas kernels  186 us (98%)
    pallas_call x1, Pallas kernels, per_device(): pl.pallas_call(functools.partial(layer_kernel, devices, planes, wide, cap...  91.4 us
    pallas_call x1, Pallas kernels, per_device(): pl.pallas_call(functools.partial(encode_kernel, devices, cap, planes), ou...  82.4 us
    pallas_call x1, Pallas kernels, per_device(): pl.pallas_call(functools.partial(place_kernel, cap, channels, per_plane),...  9.39 us

profile of v4, /device:TPU:17, one launch (start us, length us, event | category | flops | bytes accessed | tf_op | source)
XLA Modules:
  0.0 187.9 jit_solution(5202890047556480057)
XLA Ops:
  0.0 2.8 %lists.1 = (s32[128]{0:T(128)}, s32[128]{0:T(128)}, s32[64]{0:T(128)}, s32[16,8,128]{2,1,0:T(8,128)}, s32[2,128]{1,0:T(2,128)}, /*index=5*/s32[2,256]{1,0:T(2,128)}) custom-call(s32[64]{0:T(128)} %bitcast.8, s32[64]{0:T(128)} %block.1, s32[1,64]{1,0:T(1,128)} %bitcast.9, s32[1,64]{1,0:T(1,128)} %bitcast.10), custom_call_target="tpu_custom_call" | custom-call | tf_op jit(solution)/shard_map/lists/pallas_call | solution.py:774
  2.8 82.4 %encode.1 = (bf16[16,512,128]{2,1,0:T(8,128)(2,1)}, s32[16,8,128]{2,1,0:T(8,128)}, bf16[16,32,1024]{2,1,0:T(8,128)(2,1)}, bf16[512,512]{1,0:T(8,128)(2,1)}, bf16[32,512,128]{2,1,0:T(8,128)(2,1)}) custom-call(s32[128]{0:T(128)} %get-tuple-element.19.order, s32[128]{0:T(128)} %get-tuple-element.20.source, s32[16,8,128]{2,1,0:T(8,128)} %get-tuple-element.21.notes, ...), custom_call_target="tpu_custom_call" | custom-call | tf_op jit(solution)/shard_map/encode/pallas_call | solution.py:805
  85.2 9.4 %place.1 = (f32[512,4096]{1,0:T(8,128)}, bf16[16,8,64,128]{3,2,1,0:T(8,128)(2,1)}) custom-call(s32[16,8,128]{2,1,0:T(8,128)} %get-tuple-element.25.targets, bf16[16,512,128]{2,1,0:T(8,128)(2,1)} %get-tuple-element.26.got), custom_call_target="tpu_custom_call" | custom-call | tf_op jit(solution)/shard_map/place/pallas_call | solution.py:850
  94.6 91.4 %layer.1 = f32[64,2048]{1,0:T(8,128)} custom-call(s32[64]{0:T(128)} %get-tuple-element.18.slot_of, bf16[512,512]{1,0:T(8,128)(2,1)} %get-tuple-element.23.modes, bf16[32,512,128]{2,1,0:T(8,128)(2,1)} %get-tuple-element.24.table, f32[512,4096]{1,0:T(8,128)} %get-tuple-element.27.field, bf16[2,64,256]{2,1,0:T(8,128)(2,1)} %bitcast.7, ...), custom_call_target="tpu_custom_call" | custom-call | tf_op jit(solution)/shard_map/layer/pallas_call | solution.py:865
  186.1 1.9 copy.13
